TPU v7x, 32 devices: a whole 2x2x4 slice. The times are simulated.
32 devices in a mesh: lat: 8 (over y, x, core), lon: 4 (over z).
Axes of the slice: x: 2, y: 2, z: 4, core: 2. Of those that a mesh axis runs over, the one named last changes fastest.
Arguments:
- state: bfloat16 [2, 64, 256, 512], P(None, None, 'lat', 'lon'), may hold values from 3 to 5
- land_mask: int32 [256, 512], P('lat', 'lon'), may hold values from 0 to 1, as said below
- conv_weight: bfloat16 [3, 3, 64, 64], replicated, may hold values from -0.25 to 0.25
- norm_gain: float32 [64], replicated, may hold values from 0.5 to 1.5
- batchnorm_bias: float32 [64], replicated, may hold values from -0.5 to 0.5
- cotangent: bfloat16 [2, 64, 256, 512], P(None, None, 'lat', 'lon'), may hold values from -6 to 6
Outputs:
- activated: bfloat16 [2, 64, 256, 512], P(None, None, 'lat', 'lon')
- state_grad: bfloat16 [2, 64, 256, 512], P(None, None, 'lat', 'lon')
- weight_grad: float32 [3, 3, 64, 64], replicated
- gain_gradient: float32 [64], replicated
- bias_grad: float32 [64], replicated
Inputs may be any that keep to these rules, and one draw needn't show every extreme that they name: `land_mask`: ocean pixels lie in whole 32 x 32 ocean blocks, with some land pixels among them; land blocks are all 0. The first block of every region of 32 x 128 pixels is an ocean block.
All inputs are finite; a program needn't handle non-finite values.
Results may differ from a plain program's by a relative error of at most 0.00105.
The roundings to bfloat16 on the way count: a program that leaves them out, or rounds other values in their place, can miss the bound.
Values may be sent and summed in bfloat16 or wider, within the bound.
No kernel may reach another device: no remote copies, remote signals or barrier semaphores. Data moves between devices by JAX's collectives and lax.ppermute only.
A program may use at most 128 MiB of HBM per device.

v0:
```python
import functools

import jax
import jax.numpy as jnp
from jax import lax
from jax.experimental import pallas as pl
from jax.experimental.pallas import tpu as pltpu
from jax.sharding import PartitionSpec as P

F32 = jnp.float32
BF16 = jnp.bfloat16
STEP = 2
CHUNK = 16
GROUP = 4
EPS = 1e-05


def lane_of(rows, width):
    return lax.broadcasted_iota(jnp.int32, (rows, width), 1)


def rolled(value, shift, width):
    return pltpu.roll(value, lax.rem(shift + 4 * width, width), 1)


def any_lane(lane, picks):
    hit = lane == picks[0]
    for p in picks[1:]:
        hit = jnp.logical_or(hit, lane == p)
    return hit


def call(kernel, out_shape, scratch, flops, nbytes, *args, fetch=False):
    space = pl.ANY if fetch else pltpu.VMEM
    return pl.pallas_call(
        kernel,
        out_shape=out_shape,
        in_specs=[pl.BlockSpec(memory_space=space)] * len(args),
        scratch_shapes=scratch,
        compiler_params=pltpu.CompilerParams(vmem_limit_bytes=24 << 20),
        cost_estimate=pl.CostEstimate(flops=flops, bytes_accessed=nbytes, transcendentals=0),
    )(*args)


def flags(mask_ref):
    return mask_ref[...].astype(F32)


def row_lanes(h, width, count=1):
    return pl.ds(pl.multiple_of(h * width, width), count * width)


def fetches(src_ref, buf, sems):
    batch, chans = src_ref.shape[:2]
    spots = [(b, c) for b in range(batch) for c in range(0, chans, CHUNK)]
    copies = []
    for n, (b, c) in enumerate(spots):
        part = (b, pl.ds(c, CHUNK))
        copies.append(pltpu.make_async_copy(src_ref.at[part], buf.at[part], sems.at[n]))
    return spots, copies


def spread_rows(src_ref, buf, sems, mask_ref, mbuf, msem, tmp):
    batch, chans, high, width = src_ref.shape
    head = pltpu.make_async_copy(mask_ref, mbuf, msem)
    head.start()
    spots, copies = fetches(src_ref, buf, sems)
    for copy in copies:
        copy.start()
    head.wait()
    mask = flags(mbuf)
    for (b, c0), copy in zip(spots, copies):
        copy.wait()
        for c in range(c0, c0 + CHUNK):
            at = (b * chans + c) * (high + 1)
            tmp[at : at + high, :] = buf[b, c].astype(F32) * mask


def channel_rows(tmp, b, h, chans, high):
    return pl.ds(b * chans * (high + 1) + h, chans, stride=high + 1)


def pack_rows(tmp, out, chans, high):
    for c in range(chans):
        at = c * (high + 1)
        out[c] = tmp[at : at + high, :].astype(BF16)


def packed(old, v, i, lane):
    width = lane.shape[1]
    here = jnp.logical_or(lane == 2 * i, lane == lax.rem(2 * i - 1 + width, width))
    return jnp.where(here, rolled(v, 2 * i, width), old)


def gather_kernel(x_ref, mask_ref, xm_ref, top_ref, bot_ref, side_ref, tmp, buf, mbuf, sems, msem):
    batch, chans, high, width = x_ref.shape
    spread_rows(x_ref, buf, sems, mask_ref, mbuf, msem, tmp)
    lane = lane_of(chans, width)
    side = jnp.zeros((chans, width), F32)
    for b in range(batch):

        def row(h, side, b=b):
            v = tmp[channel_rows(tmp, b, h, chans, high), :]
            xm_ref[b, :, row_lanes(h, width)] = v.astype(BF16)
            return packed(side, v, b * high + h, lane)

        side = lax.fori_loop(0, high, row, side, unroll=8)
        top_ref[b] = xm_ref[b, :, 0:width]
        bot_ref[b] = xm_ref[b, :, (high - 1) * width : high * width]
    side_ref[...] = side.astype(BF16)


def relay_kernel(x_ref, mask_ref, w_hbm, out_ref, fwd_ref, back_ref, tmp, buf, mbuf, sems, msem, w_ref, wsem):
    batch, chans, high, width = x_ref.shape
    weights = pltpu.make_async_copy(w_hbm, w_ref, wsem)
    weights.start()
    spread_rows(x_ref, buf, sems, mask_ref, mbuf, msem, tmp)
    weights.wait()
    for kx in range(3):
        part = jnp.concatenate([w_ref[ky, kx].astype(F32) for ky in range(3)], axis=0)
        fwd_ref[kx * chans : (kx + 1) * chans, :] = jnp.transpose(part).astype(BF16)
        part = [w_ref[2 - ky, 2 - kx].astype(F32) for ky in range(3)]
        back_ref[kx * chans : (kx + 1) * chans, :] = jnp.concatenate(part, axis=1).astype(BF16)
    for b in range(batch):

        def row(h, carry, b=b):
            out_ref[b, :, row_lanes(h, width)] = tmp[channel_rows(tmp, b, h, chans, high), :].astype(BF16)
            return carry

        lax.fori_loop(0, high, row, 0, unroll=8)


def corners(high, batch, width):
    first = [(2 * b * high + d) % width for b in range(batch) for d in (0, -1)]
    return first, [(p + 2 * (high - 1)) % width for p in first]


def corner_kernel(high, batch, top_ref, bot_ref, fl_ref, fr_ref, edge_ref, up_ref, dn_ref):
    chans, width = fl_ref.shape
    lane = lane_of(chans, width)
    even = lax.rem(lane, 2) == 0
    edge = jnp.where(
        even, rolled(fl_ref[...].astype(F32), 1, width), rolled(fr_ref[...].astype(F32), -1, width)
    )
    first, last = corners(high, batch, width)
    far = 2 * (high - 1)
    edge_ref[...] = edge.astype(BF16)
    up = jnp.where(any_lane(lane, last), rolled(edge, far, width), 0.0)
    dn = jnp.where(any_lane(lane, first), rolled(edge, -far, width), 0.0)
    for b in range(batch):
        up_ref[b] = top_ref[b]
        dn_ref[b] = bot_ref[b]
    up_ref[batch] = up.astype(BF16)
    dn_ref[batch] = dn.astype(BF16)


def edge_stack(edge_ref, above_ref, below_ref, high, batch):
    chans, width = edge_ref.shape
    lane = lane_of(chans, width)
    edge = edge_ref[...].astype(F32)
    first, last = corners(high, batch, width)
    top = jnp.where(any_lane(lane, first), above_ref[batch].astype(F32), rolled(edge, 2, width))
    bottom = jnp.where(any_lane(lane, last), below_ref[batch].astype(F32), rolled(edge, -2, width))
    return jnp.concatenate([top, edge, bottom], axis=0).astype(BF16)


def fill_padded(pad_ref, x_ref, above_ref, below_ref, width, planes):
    flat = x_ref.shape[2]
    for to, b in enumerate(planes):
        pad_ref[to, :, 0:width] = above_ref[b]
        pad_ref[to, :, width : width + flat] = x_ref[b]
        pad_ref[to, :, width + flat :] = below_ref[b]


def taps(pad_ref, b, j, width, count):
    return jnp.concatenate([pad_ref[b, :, row_lanes(j + ky, width, count)] for ky in range(3)], axis=0)


def edge_fix(w_ref, stack, lane):
    g = jnp.dot(w_ref[...], stack, preferred_element_type=F32)
    c = g.shape[0] // 3
    return jnp.where(lax.rem(lane, 2) == 0, g[0:c], g[2 * c :])


def conv_loop(pad_ref, w_ref, bufs, fix, first, high, lane, post, carry):
    planes = pad_ref.shape[0]
    chans, width = lane.shape
    per = high // STEP
    steps = planes * per

    def product(k, buf):
        k = jnp.minimum(k, steps - 1)
        b, j = lax.div(k, per), lax.rem(k, per) * STEP
        buf[...] = jnp.dot(w_ref[...], taps(pad_ref, b, j, width, STEP), preferred_element_type=F32)

    def finish(k, buf, carry):
        b, j = lax.div(k, per), lax.rem(k, per) * STEP
        for r in range(STEP):
            cut = slice(r * width, (r + 1) * width)
            g = rolled(fix, -2 * ((first + b) * high + j + r), width)
            left = jnp.where(lane == 0, g, rolled(buf[0:chans, cut], 1, width))
            right = jnp.where(lane == width - 1, g, rolled(buf[2 * chans :, cut], -1, width))
            carry = post(b, j + r, left + buf[chans : 2 * chans, cut] + right, carry)
        return carry

    def four(p, carry):
        k = 4 * p
        product(k + 2, bufs[2])
        product(k + 3, bufs[3])
        carry = finish(k, bufs[0], carry)
        carry = finish(k + 1, bufs[1], carry)
        product(k + 4, bufs[0])
        product(k + 5, bufs[1])
        carry = finish(k + 2, bufs[2], carry)
        return finish(k + 3, bufs[3], carry)

    product(0, bufs[0])
    product(1, bufs[1])
    return lax.fori_loop(0, steps // 4, four, carry)


def lanes_sum(first, second):
    both = jnp.concatenate([first, second], axis=0)
    return jnp.sum(jnp.transpose(both), axis=0, keepdims=True)


def conv_kernel(
    x_ref, above_ref, below_ref, edge_ref, w_ref, mask_ref,
    conv_ref, pad_ref, stack_ref, stat_ref, maskf, *bufs,
):
    batch, chans, flat = x_ref.shape
    high, width = mask_ref.shape
    lane = lane_of(chans, width)
    maskf[...] = flags(mask_ref)
    fill_padded(pad_ref, x_ref, above_ref, below_ref, width, range(batch))
    stack = edge_stack(edge_ref, above_ref, below_ref, high, batch)
    stack_ref[...] = stack
    fix = edge_fix(w_ref, stack, lane)

    def post(b, h, value, total):
        conv_ref[b, :, row_lanes(h, width)] = value
        return total + value * maskf[pl.ds(h, 1), :]

    zero = jnp.zeros((chans, width), F32)
    total = conv_loop(pad_ref, w_ref, bufs, fix, 0, high, lane, post, zero)
    n = batch * jnp.sum(maskf[...])
    mean = jnp.sum(total, axis=1, keepdims=True) / jnp.maximum(n, 1.0)
    mean = jnp.broadcast_to(mean, (chans, width))
    spread = zero
    for b in range(batch):

        def step(h, spread, b=b):
            dev = conv_ref[b, :, row_lanes(h, width)] - mean
            return spread + dev * dev * maskf[pl.ds(h, 1), :]

        spread = lax.fori_loop(0, high, step, spread, unroll=8)
    copies = stat_ref.shape[0]
    stat_ref[:, 0:1, :] = jnp.broadcast_to(lanes_sum(total, spread)[None], (copies, 1, 2 * chans))
    stat_ref[:, 1:2, :] = jnp.full((copies, 1, 2 * chans), n, F32)


def columns(rows, chans):
    width = rows[0].shape[1]
    pad = jnp.zeros((width - len(rows), width), F32)
    return jnp.transpose(jnp.concatenate(rows + [pad], axis=0))[0:chans]


def column(cols, k, width):
    return jnp.broadcast_to(cols[:, k : k + 1], (cols.shape[0], width))


def widened(row, width):
    return jnp.concatenate([row, jnp.zeros((1, width - row.shape[1]), F32)], axis=1)


def silu_kernel(
    stat_ref, conv_ref, cot_ref, mask_ref, gain_ref, bias_ref, act_ref, dpre_ref, par_ref, sum_ref, maskf, tmp
):
    batch, chans, flat = conv_ref.shape
    high, width = mask_ref.shape
    maskf[...] = flags(mask_ref)
    stat = stat_ref[:, 0, :]
    n = stat_ref[:, 1, :]
    count = jnp.maximum(jnp.sum(n, axis=0, keepdims=True), 1.0)
    both = jnp.sum(stat, axis=0, keepdims=True)
    mean = both / count
    off = stat / jnp.maximum(n, 1.0) - mean
    between = jnp.sum(n * off * off, axis=0, keepdims=True)
    var = (rolled(both, chans, width) + between) / count
    inv = lax.rsqrt(var + EPS)
    gain = widened(gain_ref[...], width)
    bias = widened(bias_ref[...], width)
    cols = columns([mean, inv, gain, 0.5 * gain * inv, 0.5 * bias, count], chans)
    par_ref[...] = cols
    mean, slope, shift = (column(cols, k, width) for k in (0, 3, 4))
    sums = (jnp.zeros((chans, width), F32), jnp.zeros((chans, width), F32))
    for b in range(batch):

        def row(h, sums, b=b):
            at = row_lanes(h, width)
            dev = conv_ref[b, :, at] - mean
            half = slope * dev + shift
            t = jnp.tanh(half)
            s = 0.5 + 0.5 * t
            act = half + half * t
            tmp[channel_rows(tmp, b, h, chans, high), :] = act * maskf[pl.ds(h, 1), :]
            dpre = cot_ref[b, :, at].astype(F32) * (s + act * (0.5 - 0.5 * t))
            dpre_ref[b, :, at] = dpre
            return sums[0] + dpre, sums[1] + dpre * dev

        sums = lax.fori_loop(0, high, row, sums, unroll=4)
    total = lanes_sum(sums[0], sums[1] * column(cols, 1, width))
    sum_ref[...] = jnp.broadcast_to(total[None], sum_ref.shape)
    for b in range(batch):
        pack_rows(tmp.at[b * chans * (high + 1) : (b + 1) * chans * (high + 1)], act_ref.at[b], chans, high)


def grad_kernel(
    sum_ref, conv_ref, dpre_ref, par_ref, pad_ref, stack_ref, mask_ref,
    d_ref, top_ref, bot_ref, side_ref, out_ref, bg_ref, gg_ref, maskf, acc, da, db, wg_ref,
):
    batch, chans, flat = conv_ref.shape
    high, width = mask_ref.shape
    lane = lane_of(chans, width)
    maskf[...] = flags(mask_ref)
    both = jnp.sum(sum_ref[:, 0, :], axis=0, keepdims=True)
    bg_ref[...] = both[:, 0:chans]
    gg_ref[...] = both[:, chans : 2 * chans]
    cols = par_ref[...]
    mean, inv, gain, count = (column(cols, k, width) for k in (0, 1, 2, 5))
    sums = columns([both], 2 * chans)
    scale = gain * inv
    first = scale * column(sums[0:chans], 0, width) / count
    second = scale * inv * column(sums[chans:], 0, width) / count
    acc[...] = jnp.zeros_like(acc)
    contract = (((1,), (1,)), ((), ()))
    per = high // GROUP
    steps = batch * per

    def place(k):
        return lax.div(k, per), lax.rem(k, per) * GROUP

    def build(k, buf, side):
        b, j = place(k)
        for r in range(GROUP):
            h = j + r
            at = row_lanes(h, width)
            dev = conv_ref[b, :, at] - mean
            d = (maskf[pl.ds(h, 1), :] * (scale * dpre_ref[b, :, at] - first - dev * second)).astype(BF16)
            d_ref[b, :, at] = d
            v = d.astype(F32)
            side = packed(side, v, b * high + h, lane)
            cut = slice(r * width, (r + 1) * width)
            buf[0:chans, cut] = jnp.where(lane == width - 1, 0.0, rolled(v, -1, width)).astype(BF16)
            buf[chans : 2 * chans, cut] = d
            buf[2 * chans :, cut] = jnp.where(lane == 0, 0.0, rolled(v, 1, width)).astype(BF16)
        return side

    def product(k, buf):
        b, j = place(k)
        rhs = buf[...]
        return lax.dot_general(taps(pad_ref, b, j, width, GROUP), rhs, contract, preferred_element_type=F32)

    def pair(p, side):
        k = 2 * p
        gain = product(k, da)
        side = build(k + 1, db, side)
        acc[...] += gain
        gain = product(k + 1, db)
        side = build(jnp.minimum(k + 2, steps - 1), da, side)
        acc[...] += gain
        return side

    side = build(0, da, jnp.zeros((chans, width), F32))
    side = lax.fori_loop(0, steps // 2, pair, side)
    for b in range(batch):
        top_ref[b] = d_ref[b, :, 0:width]
        bot_ref[b] = d_ref[b, :, (high - 1) * width : high * width]
    side_ref[...] = side.astype(BF16)
    even = lax.rem(lane, 2) == 0
    zero = jnp.zeros((chans, width), F32)
    rim = jnp.concatenate([jnp.where(even, side, 0.0), zero, jnp.where(even, 0.0, side)], axis=0)
    full = acc[...] + lax.dot_general(
        stack_ref[...], rim.astype(BF16), contract, preferred_element_type=F32
    )
    half = 3 * chans // 2
    wg_ref[0 : 3 * chans, :] = full[:, 0 : 2 * chans]
    wg_ref[3 * chans : 3 * chans + half, :] = jnp.concatenate(
        [full[0:half, 2 * chans :], full[half:, 2 * chans :]], axis=1
    )
    share = out_ref.shape[1]
    if wg_ref.shape[0] > 3 * chans + half:
        wg_ref[3 * chans + half :, :] = jnp.zeros((wg_ref.shape[0] - 3 * chans - half, width), F32)
    for p in range(out_ref.shape[0]):
        out_ref[p] = wg_ref[p * share : (p + 1) * share, :]


def total_kernel(x_ref, out_ref):
    total = jnp.sum(x_ref[...], axis=0, keepdims=True)
    out_ref[...] = jnp.broadcast_to(total, out_ref.shape)


def unpack_kernel(chans, x_ref, out_ref, wg_ref):
    half = 3 * chans // 2
    share = x_ref.shape[1]
    for p in range(x_ref.shape[0]):
        wg_ref[p * share : (p + 1) * share, :] = x_ref[p]
    for ky in range(3):
        for kx in range(2):
            out_ref[ky, kx] = wg_ref[ky * chans : (ky + 1) * chans, kx * chans : (kx + 1) * chans]
    tail = jnp.concatenate(
        [
            wg_ref[3 * chans : 3 * chans + half, 0:chans],
            wg_ref[3 * chans : 3 * chans + half, chans : 2 * chans],
        ],
        axis=0,
    )
    for ky in range(3):
        out_ref[ky, 2] = tail[ky * chans : (ky + 1) * chans]


def back_kernel(plane, d_ref, above_ref, below_ref, edge_ref, w_ref, mask_ref, *rest):
    out_ref, pad_ref, maskf, tmp, *bufs, tile, sem = rest[-10:]
    batch, chans, flat = d_ref.shape
    high, width = mask_ref.shape
    lane = lane_of(chans, width)
    maskf[...] = flags(mask_ref)
    fill_padded(pad_ref, d_ref, above_ref, below_ref, width, [plane])
    fix = edge_fix(w_ref, edge_stack(edge_ref, above_ref, below_ref, high, batch), lane)

    def post(b, h, value, carry):
        tmp[channel_rows(tmp, 0, h, chans, high), :] = value * maskf[pl.ds(h, 1), :]
        return carry

    conv_loop(pad_ref, w_ref, bufs, fix, plane, high, lane, post, 0)
    pack_rows(tmp, tile, chans, high)
    copy = pltpu.make_async_copy(tile, out_ref.at[plane], sem)
    copy.start()
    copy.wait()


def neighbours(axis, ring):
    n = lax.axis_size(axis)
    even = [(i, i ^ 1) for i in range(n)]
    odd = [(i, (i + 1) % n if i % 2 else (i - 1) % n) for i in range(n)]
    if not ring:
        odd = [pair for pair in odd if pair not in ((0, n - 1), (n - 1, 0))]
    return even, odd


def lon_swap(side):
    n = lax.axis_size("lon")
    if n % 2:
        from_left = lax.ppermute(side, "lon", [(i, (i + 1) % n) for i in range(n)])
        from_right = lax.ppermute(side, "lon", [((i + 1) % n, i) for i in range(n)])
        return from_left, from_right
    even, odd = neighbours("lon", True)
    first = lax.ppermute(side, "lon", even)
    second = lax.ppermute(side, "lon", odd)
    flag = lax.axis_index("lon") % 2 == 1
    return jnp.where(flag, first, second), jnp.where(flag, second, first)


def lat_swap(up, dn):
    n = lax.axis_size("lat")
    if n % 2:
        above = lax.ppermute(dn, "lat", [(i, i + 1) for i in range(n - 1)])
        below = lax.ppermute(up, "lat", [(i + 1, i) for i in range(n - 1)])
        return above, below
    even, odd = neighbours("lat", False)
    flag = lax.axis_index("lat") % 2 == 1
    second = lax.ppermute(jnp.where(flag, dn, up), "lat", odd)
    first = lax.ppermute(jnp.where(flag, up, dn), "lat", even)
    return jnp.where(flag, first, second), jnp.where(flag, second, first)


def with_corners(top, bot, sides, high):
    batch, chans, width = top.shape
    shapes = (
        jax.ShapeDtypeStruct((chans, width), BF16),
        jax.ShapeDtypeStruct((batch + 1, chans, width), BF16),
        jax.ShapeDtypeStruct((batch + 1, chans, width), BF16),
    )
    return call(functools.partial(corner_kernel, high, batch), shapes, [], 0, 200_000, top, bot, *sides)


def on_device(state, land_mask, conv_weight, norm_gain, batchnorm_bias, cotangent):
    batch, chans, high, width = state.shape
    flat = high * width
    axes = ("lat", "lon")
    devices = lax.axis_size(axes)
    S = jax.ShapeDtypeStruct
    mat = 2 * batch * flat * 9 * chans * chans
    size = batch * chans * flat * 2
    tmp = pltpu.VMEM((batch * chans * (high + 1), width), F32)
    maskf = pltpu.VMEM((high, width), F32)
    products = [pltpu.VMEM((3 * chans, STEP * width), F32)] * 4
    plane = S((batch, chans, flat), BF16)
    wide = S((batch, chans, flat), F32)
    rows = S((batch, chans, width), BF16)
    cols = S((chans, width), BF16)
    square = S((3 * chans, 3 * chans), BF16)
    incoming = [
        tmp,
        pltpu.VMEM(state.shape, BF16),
        pltpu.VMEM(land_mask.shape, jnp.int32),
        pltpu.SemaphoreType.DMA((batch * chans // CHUNK,)),
        pltpu.SemaphoreType.DMA,
    ]
    weights = [pltpu.VMEM(conv_weight.shape, BF16), pltpu.SemaphoreType.DMA]
    xm, top, bot, side = call(
        gather_kernel, (plane, rows, rows, cols), incoming, 0, 2 * size, state, land_mask, fetch=True
    )
    cot, w_fwd, w_back = call(
        relay_kernel, (plane, square, square), incoming + weights, 0, 2 * size,
        cotangent, land_mask, conv_weight, fetch=True,
    )
    edge, up, dn = with_corners(top, bot, lon_swap(side), high)
    above, below = lat_swap(up, dn)
    conv, padded, stack, stat = call(
        conv_kernel,
        (
            wide,
            S((batch, chans, flat + 2 * width), BF16),
            S((3 * chans, width), BF16),
            S((devices, 2, 2 * chans), F32),
        ),
        [maskf] + products,
        4 * mat,
        4 * size,
        xm, above, below, edge, w_fwd, land_mask,
    )
    stats = lax.all_to_all(stat, axes, 0, 0)
    activated, dpre, par, sums = call(
        silu_kernel,
        (S(state.shape, BF16), wide, S((chans, width), F32), S((devices, 1, 2 * chans), F32)),
        [maskf, tmp],
        20 * size,
        6 * size,
        stats, conv, cot, land_mask, norm_gain[None], batchnorm_bias[None],
    )
    sums = lax.all_to_all(sums, axes, 0, 0)
    stacked = pltpu.VMEM((3 * chans, GROUP * width), BF16)
    share = -(-9 * chans * chans // (width * devices))
    flatg = pltpu.VMEM((share * devices, width), F32)
    dmap, top, bot, side, wg, bg, gg = call(
        grad_kernel,
        (
            plane, rows, rows, cols,
            S((devices, share, width), F32), S((1, chans), F32), S((1, chans), F32),
        ),
        [maskf, pltpu.VMEM((3 * chans, 3 * chans), F32), stacked, stacked, flatg],
        4 * mat,
        6 * size,
        sums, conv, dpre, par, padded, stack, land_mask,
    )

    parts = lax.all_to_all(wg, axes, 0, 0)
    edge, up, dn = with_corners(top, bot, lon_swap(side), high)
    above, below = lat_swap(up, dn)
    parts, above, below, edge = lax.optimization_barrier((parts, above, below, edge))
    shares = call(total_kernel, S((devices, share, width), F32), [], 0, 600_000, parts)
    wg = lax.all_to_all(shares, axes, 0, 0)

    def backward(b, earlier):
        kept = {} if earlier is None else {"input_output_aliases": {6: 0}}
        whole = pl.BlockSpec(memory_space=pltpu.VMEM)
        far = pl.BlockSpec(memory_space=pl.ANY)
        extra = [] if earlier is None else [earlier]
        return pl.pallas_call(
            functools.partial(back_kernel, b),
            out_shape=S(state.shape, BF16),
            in_specs=[whole] * 6 + [far] * len(extra),
            out_specs=far,
            scratch_shapes=[
                pltpu.VMEM((1, chans, flat + 2 * width), BF16),
                maskf,
                pltpu.VMEM((chans * (high + 1), width), F32),
            ]
            + products
            + [pltpu.VMEM((chans, high, width), BF16), pltpu.SemaphoreType.DMA],
            compiler_params=pltpu.CompilerParams(vmem_limit_bytes=24 << 20),
            cost_estimate=pl.CostEstimate(flops=2 * mat, bytes_accessed=2 * size, transcendentals=0),
            **kept,
        )(dmap, above, below, edge, w_back, land_mask, *extra)

    state_grad = None
    for b in range(batch):
        state_grad = backward(b, state_grad)
    weight_grad = call(
        functools.partial(unpack_kernel, chans), S((3, 3, chans, chans), F32), [flatg], 0, 500_000, wg
    )
    return (activated, state_grad, weight_grad, gg[0], bg[0])


def solution(mesh):
    return jax.shard_map(
        on_device,
        mesh=mesh,
        in_specs=(
            P(None, None, "lat", "lon"),
            P("lat", "lon"),
            P(),
            P(),
            P(),
            P(None, None, "lat", "lon"),
        ),
        out_specs=(P(None, None, "lat", "lon"), P(None, None, "lat", "lon"), P(), P(), P()),
        check_vma=False,
    )
```

profile of v0, /device:TPU:0, one launch (start us, length us, event | category | flops | bytes accessed | tf_op | source)
XLA Modules:
  0.0 81.6 jit_solution(2610669319085247396)
XLA Ops:
  0.6 0.0 copy-start
  0.6 0.0 copy-start.1
  0.7 1.3 %copy-done.1 = bf16[2,64,32,128]{3,2,1,0:T(8,128)(2,1)S(1)} copy-done((bf16[2,64,32,128]{3,2,1,0:T(8,128)(2,1)S(1)}, bf16[2,64,32,128]{3,2,1,0:T(8,128)(2,1)}, u32[]{:S(2)}) %copy-start.1) | copy-done | bytes 1048600
  2.0 0.0 copy-start.2
  2.0 0.7 copy-done.2
  2.7 0.0 copy-start.4
  2.7 2.8 %shard_map.101 = (bf16[2,64,4096]{2,1,0:T(8,128)(2,1)S(1)}, bf16[2,64,128]{2,1,0:T(8,128)(2,1)S(1)}, bf16[2,64,128]{2,1,0:T(8,128)(2,1)S(1)}, bf16[64,128]{1,0:T(8,128)(2,1)S(1)}) custom-call(bf16[2,64,32,128]{3,2,1,0:T(8,128)(2,1)S(1)} %copy-done.1, s32[32,128]{1,0:T(8,128)S(1)} %copy-done.2), custom_call_target="tpu_custom_call" | custom-call | bytes 2097152 | tf_op jit(solution)/shard_map/pallas_call | solution.py:35
  5.5 5.1 %collective-permute-start.1 = (bf16[64,128]{1,0:T(8,128)(2,1)S(1)}, bf16[64,128]{1,0:T(8,128)(2,1)S(1)}, u32[]{:S(2)}, u32[]{:S(2)}) collective-permute-start(bf16[64,128]{1,0:T(8,128)(2,1)S(1)} %get-tuple-element.40), channel_id=1, source_target_pairs={{0,3},{1,2},{2,1},{3,0},{4,7},{5,6},{6,5},{7,4},{8,11},{9,10},{10,... | collective-permute-start | bytes 49160 | tf_op jit(solution)/shard_map/ppermute | solution.py:459
  10.6 0.0 collective-permute-start
  10.6 1.7 %collective-permute-done.1 = bf16[64,128]{1,0:T(8,128)(2,1)S(1)} collective-permute-done((bf16[64,128]{1,0:T(8,128)(2,1)S(1)}, bf16[64,128]{1,0:T(8,128)(2,1)S(1)}, u32[]{:S(2)}, u32[]{:S(2)}) %collective-permute-start.1) | collective-permute-done | bytes 16416 | tf_op jit(solution)/shard_map/ppermute | solution.py:459
  12.4 2.0 %collective-permute-done = bf16[64,128]{1,0:T(8,128)(2,1)S(1)} collective-permute-done((bf16[64,128]{1,0:T(8,128)(2,1)S(1)}, bf16[64,128]{1,0:T(8,128)(2,1)S(1)}, u32[]{:S(2)}, u32[]{:S(2)}) %collective-permute-start) | collective-permute-done | bytes 16416 | tf_op jit(solution)/shard_map/ppermute | solution.py:458
  14.4 0.2 shard_map.102
  14.6 0.7 collective-permute-start.3
  15.2 2.9 %collective-permute-start.2 = (bf16[3,64,128]{2,1,0:T(8,128)(2,1)S(1)}, bf16[3,64,128]{2,1,0:T(8,128)(2,1)S(1)}, u32[]{:S(2)}, u32[]{:S(2)}) collective-permute-start(bf16[3,64,128]{2,1,0:T(8,128)(2,1)S(1)} %get-tuple-element.76), channel_id=1, source_target_pairs={{0,4},{4,0},{8,12},{12,8},{16,20},{20,16},{24,28},{28,24},{1,5},{5... | collective-permute-start | bytes 147464 | tf_op jit(solution)/shard_map/ppermute | solution.py:473
  18.1 0.0 copy-done
  18.1 0.0 copy-start.3
  18.1 0.7 copy-done.3
  18.9 0.0 copy-start.5
  18.9 0.9 %copy-done.5 = bf16[3,3,64,64]{3,2,1,0:T(8,128)(2,1)S(1)} copy-done((bf16[3,3,64,64]{3,2,1,0:T(8,128)(2,1)S(1)}, bf16[3,3,64,64]{3,2,1,0:T(8,128)(2,1)}, u32[]{:S(2)}) %copy-start.5) | copy-done | bytes 73752
  19.8 2.1 %shard_map.103 = (bf16[2,64,4096]{2,1,0:T(8,128)(2,1)S(1)}, bf16[192,192]{1,0:T(8,128)(2,1)S(1)}, bf16[192,192]{1,0:T(8,128)(2,1)S(1)}) custom-call(bf16[2,64,32,128]{3,2,1,0:T(8,128)(2,1)S(1)} %copy-done, s32[32,128]{1,0:T(8,128)S(1)} %copy-done.3, bf16[3,3,64,64]{3,2,1,0:T(8,128)(2,1)S(1)} %copy-done.5), custom_call_target="tpu_custom_call" | custom-call | bytes 2097152 | tf_op jit(solution)/shard_map/pallas_call | solution.py:35
  21.9 0.0 collective-permute-done.3
  21.9 0.0 collective-permute-done.2
  22.0 0.0 copy-done.4
  22.0 0.0 copy-start.6
  22.0 0.0 copy-start.7
  22.0 3.5 %shard_map.104 = (f32[2,64,4096]{2,1,0:T(8,128)S(1)}, bf16[2,64,4352]{2,1,0:T(8,128)(2,1)S(1)}, bf16[192,128]{1,0:T(8,128)(2,1)S(1)}, f32[32,2,128]{2,1,0:T(2,128)S(1)}) custom-call(bf16[2,64,4096]{2,1,0:T(8,128)(2,1)S(1)} %get-tuple-element.37.x_ref, bf16[3,64,128]{2,1,0:T(8,128)(2,1)S(1)} %get-tuple-element.74.above_ref, ...), custom_call_target="tpu_custom_call" | custom-call | flops 2415919104 | bytes 4194304 | tf_op jit(solution)/shard_map/pallas_call | solution.py:35
  25.5 10.2 %all_to_all.20.stat_ref = f32[32,2,128]{2,1,0:T(2,128)S(1)} all-to-all(f32[32,2,128]{2,1,0:T(2,128)S(1)} %get-tuple-element.45), channel_id=1, replica_groups=mesh['lat'=8,'lon'=4] {'lat','lon'}, dimensions={0} | all-to-all | bytes 65536 | tf_op jit(solution)/shard_map/all_to_all | solution.py:533
  35.7 0.0 copy-done.6
  35.7 0.0 copy-done.7
  35.7 2.9 %shard_map.105 = (bf16[2,64,32,128]{3,2,1,0:T(8,128)(2,1)}, f32[2,64,4096]{2,1,0:T(8,128)S(1)}, f32[64,128]{1,0:T(8,128)S(1)}, f32[32,1,128]{2,1,0:T(1,128)S(1)}) custom-call(f32[32,2,128]{2,1,0:T(2,128)S(1)} %all_to_all.20.stat_ref, f32[2,64,4096]{2,1,0:T(8,128)S(1)} %get-tuple-element.46.conv_ref, bf16[2,64,4096]{2,1,0:T(8,128)(2,1)S(1)} %get-tuple-element.47.cot_ref, ...), custom_call_target="tpu_custom_call" | custom-call | flops 20971520 | bytes 6291456 | tf_op jit(solution)/shard_map/pallas_call | solution.py:35
  38.6 8.9 %all_to_all.21.sum_ref = f32[32,1,128]{2,1,0:T(1,128)S(1)} all-to-all(f32[32,1,128]{2,1,0:T(1,128)S(1)} %get-tuple-element.49), channel_id=1, replica_groups=mesh['lat'=8,'lon'=4] {'lat','lon'}, dimensions={0} | all-to-all | bytes 32768 | tf_op jit(solution)/shard_map/all_to_all | solution.py:542
  47.5 4.6 %shard_map.106 = (bf16[2,64,4096]{2,1,0:T(8,128)(2,1)S(1)}, bf16[2,64,128]{2,1,0:T(8,128)(2,1)S(1)}, bf16[2,64,128]{2,1,0:T(8,128)(2,1)S(1)}, bf16[64,128]{1,0:T...) custom-call(f32[32,1,128]{2,1,0:T(1,128)S(1)} %all_to_all.21.sum_ref, ...), custom_call_target="tpu_custom_call" | custom-call | flops 2415919104 | bytes 6291456 | tf_op jit(solution)/shard_map/pallas_call | solution.py:35
  52.1 0.6 collective-permute-start.5
  52.6 0.5 collective-permute-start.4
  53.2 3.7 %all-to-all-start.2 = ((f32[32,9,128]{2,1,0:T(8,128)}), f32[32,9,128]{2,1,0:T(8,128)S(1)}, u32[]{:S(2)}, u32[]{:S(2)}) async-start(f32[32,9,128]{2,1,0:T(8,128)} %get-tuple-element.55), calls=%async_computation.2 | async-start | bytes 524288 | tf_op jit(solution)/shard_map/all_to_all | solution.py:558
  56.9 0.7 collective-permute-done.5
  57.6 0.0 collective-permute-done.4
  57.6 0.2 shard_map.107
  57.8 0.7 collective-permute-start.7
  58.5 2.5 %collective-permute-start.6 = (bf16[3,64,128]{2,1,0:T(8,128)(2,1)S(1)}, bf16[3,64,128]{2,1,0:T(8,128)(2,1)S(1)}, u32[]{:S(2)}, u32[]{:S(2)}) collective-permute-start(bf16[3,64,128]{2,1,0:T(8,128)(2,1)S(1)} %get-tuple-element.72), channel_id=1, source_target_pairs={{0,4},{4,0},{8,12},{12,8},{16,20},{20,16},{24,28},{28,24},{1,5},{5... | collective-permute-start | bytes 147464 | tf_op jit(solution)/shard_map/ppermute | solution.py:473
  61.0 0.0 collective-permute-done.7
  61.0 0.9 %collective-permute-done.6 = bf16[3,64,128]{2,1,0:T(8,128)(2,1)S(1)} collective-permute-done((bf16[3,64,128]{2,1,0:T(8,128)(2,1)S(1)}, bf16[3,64,128]{2,1,0:T(8,128)(2,1)S(1)}, u32[]{:S(2)}, u32[]{:S(2)}) %collective-permute-start.6) | collective-permute-done | bytes 49184 | tf_op jit(solution)/shard_map/ppermute | solution.py:473
  61.9 5.3 %all-to-all-done.2.x_ref = f32[32,9,128]{2,1,0:T(8,128)S(1)} async-done(((f32[32,9,128]{2,1,0:T(8,128)}), f32[32,9,128]{2,1,0:T(8,128)S(1)}, u32[]{:S(2)}, u32[]{:S(2)}) %all-to-all-start.2) | async-done | bytes 147488 | tf_op jit(solution)/shard_map/all_to_all | solution.py:558
  67.1 0.8 shard_map.110
  67.9 2.7 %all-to-all-start.3 = ((f32[32,9,128]{2,1,0:T(8,128)}), f32[32,9,128]{2,1,0:T(8,128)S(1)}, u32[]{:S(2)}, u32[]{:S(2)}) async-start(f32[32,9,128]{2,1,0:T(8,128)} %shard_map.110), calls=%async_computation.3 | async-start | bytes 524288 | tf_op jit(solution)/shard_map/all_to_all | solution.py:563
  70.5 2.4 %shard_map.108.rest_0_ = bf16[2,64,32,128]{3,2,1,0:T(8,128)(2,1)} custom-call(bf16[2,64,4096]{2,1,0:T(8,128)(2,1)S(1)} %get-tuple-element.54.d_ref, bf16[3,64,128]{2,1,0:T(8,128)(2,1)S(1)} %get-tuple-element.62.above_ref, bf16[3,64,128]{2,1,0:T(8,128)(2,1)S(1)} %get-tuple-element.63.below_ref, bf16[64,128]{1,0:T(8,128)(2,1)S(1)} %get-tuple-element.64.edge_ref, ...), custom_call_target="tpu_custom_call" | custom-call | flops 1207959552 | bytes 2097152 | tf_op jit(solution)/shard_map/pallas_call | solution.py:570
  73.0 2.5 %shard_map.109 = bf16[2,64,32,128]{3,2,1,0:T(8,128)(2,1)} custom-call(bf16[2,64,4096]{2,1,0:T(8,128)(2,1)S(1)} %get-tuple-element.54.d_ref, bf16[3,64,128]{2,1,0:T(8,128)(2,1)S(1)} %get-tuple-element.62.above_ref, bf16[3,64,128]{2,1,0:T(8,128)(2,1)S(1)} %get-tuple-element.63.below_ref, ...), custom_call_target="tpu_custom_call", output_to_operand_aliasing={{}: (6, {})} | custom-call | flops 1207959552 | bytes 2097152 | tf_op jit(solution)/shard_map/pallas_call | solution.py:570
  75.5 5.3 %all-to-all-done.3.x_ref = f32[32,9,128]{2,1,0:T(8,128)S(1)} async-done(((f32[32,9,128]{2,1,0:T(8,128)}), f32[32,9,128]{2,1,0:T(8,128)S(1)}, u32[]{:S(2)}, u32[]{:S(2)}) %all-to-all-start.3) | async-done | bytes 147488 | tf_op jit(solution)/shard_map/all_to_all | solution.py:563
  80.8 0.8 %shard_map.111 = f32[3,3,64,64]{3,2,1,0:T(8,128)} custom-call(f32[32,9,128]{2,1,0:T(8,128)S(1)} %all-to-all-done.3.x_ref), custom_call_target="tpu_custom_call" | custom-call | bytes 500000 | tf_op jit(solution)/shard_map/pallas_call | solution.py:35
  (6 shorter events, 0.1 us)
Async XLA Ops:
  0.6 17.5 %copy-start = (bf16[2,64,32,128]{3,2,1,0:T(8,128)(2,1)S(1)}, bf16[2,64,32,128]{3,2,1,0:T(8,128)(2,1)}, u32[]{:S(2)}) copy-start(bf16[2,64,32,128]{3,2,1,0:T(8,128)(2,1)} %x_ref.3) | copy-start | bytes 3145732
  0.6 1.3 %copy-start.1 = (bf16[2,64,32,128]{3,2,1,0:T(8,128)(2,1)S(1)}, bf16[2,64,32,128]{3,2,1,0:T(8,128)(2,1)}, u32[]{:S(2)}) copy-start(bf16[2,64,32,128]{3,2,1,0:T(8,128)(2,1)} %x_ref.2) | copy-start | bytes 3145732
  2.0 0.7 copy-start.2
  2.7 19.3 %copy-start.4 = (s32[32,128]{1,0:T(8,128)S(1)}, s32[32,128]{1,0:T(8,128)}, u32[]{:S(2)}) copy-start(s32[32,128]{1,0:T(8,128)} %mask_ref.13) | copy-start | bytes 49156
  5.5 6.9 %collective-permute-start.1 = (bf16[64,128]{1,0:T(8,128)(2,1)S(1)}, bf16[64,128]{1,0:T(8,128)(2,1)S(1)}, u32[]{:S(2)}, u32[]{:S(2)}) collective-permute-start(bf16[64,128]{1,0:T(8,128)(2,1)S(1)} %get-tuple-element.40), channel_id=1, source_target_pairs={{0,3},{1,2},{2,1},{3,0},{4,7},{5,6},{6,5},{7,4},{8,11},{9,10},{10,... | collective-permute-start | bytes 49160 | tf_op jit(solution)/shard_map/ppermute | solution.py:459
  10.6 3.7 %collective-permute-start = (bf16[64,128]{1,0:T(8,128)(2,1)S(1)}, bf16[64,128]{1,0:T(8,128)(2,1)S(1)}, u32[]{:S(2)}, u32[]{:S(2)}) collective-permute-start(bf16[64,128]{1,0:T(8,128)(2,1)S(1)} %get-tuple-element.40), channel_id=1, source_target_pairs={{0,1},{1,0},{2,3},{3,2},{4,5},{5,4},{6,7},{7,6},{8,9},{9,8},{10,11... | collective-permute-start | bytes 49160 | tf_op jit(solution)/shard_map/ppermute | solution.py:458
  14.6 7.4 %collective-permute-start.3 = (bf16[3,64,128]{2,1,0:T(8,128)(2,1)S(1)}, bf16[3,64,128]{2,1,0:T(8,128)(2,1)S(1)}, u32[]{:S(2)}, u32[]{:S(2)}) collective-permute-start(bf16[3,64,128]{2,1,0:T(8,128)(2,1)S(1)} %get-tuple-element.75), channel_id=1, source_target_pairs={{4,8},{8,4},{12,16},{16,12},{20,24},{24,20},{5,9},{9,5},{13,17},{1... | collective-permute-start | bytes 147464 | tf_op jit(solution)/shard_map/ppermute | solution.py:472
  15.2 6.7 %collective-permute-start.2 = (bf16[3,64,128]{2,1,0:T(8,128)(2,1)S(1)}, bf16[3,64,128]{2,1,0:T(8,128)(2,1)S(1)}, u32[]{:S(2)}, u32[]{:S(2)}) collective-permute-start(bf16[3,64,128]{2,1,0:T(8,128)(2,1)S(1)} %get-tuple-element.76), channel_id=1, source_target_pairs={{0,4},{4,0},{8,12},{12,8},{16,20},{20,16},{24,28},{28,24},{1,5},{5... | collective-permute-start | bytes 147464 | tf_op jit(solution)/shard_map/ppermute | solution.py:473
  18.1 0.7 copy-start.3
  18.9 0.9 %copy-start.5 = (bf16[3,3,64,64]{3,2,1,0:T(8,128)(2,1)S(1)}, bf16[3,3,64,64]{3,2,1,0:T(8,128)(2,1)}, u32[]{:S(2)}) copy-start(bf16[3,3,64,64]{3,2,1,0:T(8,128)(2,1)} %w_hbm.1) | copy-start | bytes 221188
  22.0 13.7 %copy-start.6 = (f32[64]{0:T(128)S(1)}, f32[64]{0:T(128)}, u32[]{:S(2)}) copy-start(f32[64]{0:T(128)} %param.9) | copy-start | bytes 772
  22.0 13.7 %copy-start.7 = (f32[64]{0:T(128)S(1)}, f32[64]{0:T(128)}, u32[]{:S(2)}) copy-start(f32[64]{0:T(128)} %param.10) | copy-start | bytes 772
  52.1 5.5 %collective-permute-start.5 = (bf16[64,128]{1,0:T(8,128)(2,1)S(1)}, bf16[64,128]{1,0:T(8,128)(2,1)S(1)}, u32[]{:S(2)}, u32[]{:S(2)}) collective-permute-start(bf16[64,128]{1,0:T(8,128)(2,1)S(1)} %get-tuple-element.58), channel_id=1, source_target_pairs={{0,3},{1,2},{2,1},{3,0},{4,7},{5,6},{6,5},{7,4},{8,11},{9,10},{10,... | collective-permute-start | bytes 49160 | tf_op jit(solution)/shard_map/ppermute | solution.py:459
  52.6 5.0 %collective-permute-start.4 = (bf16[64,128]{1,0:T(8,128)(2,1)S(1)}, bf16[64,128]{1,0:T(8,128)(2,1)S(1)}, u32[]{:S(2)}, u32[]{:S(2)}) collective-permute-start(bf16[64,128]{1,0:T(8,128)(2,1)S(1)} %get-tuple-element.58), channel_id=1, source_target_pairs={{0,1},{1,0},{2,3},{3,2},{4,5},{5,4},{6,7},{7,6},{8,9},{9,8},{10,11... | collective-permute-start | bytes 49160 | tf_op jit(solution)/shard_map/ppermute | solution.py:458
  53.2 13.9 %all-to-all-start.2 = ((f32[32,9,128]{2,1,0:T(8,128)}), f32[32,9,128]{2,1,0:T(8,128)S(1)}, u32[]{:S(2)}, u32[]{:S(2)}) async-start(f32[32,9,128]{2,1,0:T(8,128)} %get-tuple-element.55), calls=%async_computation.2 | async-start | bytes 524288 | tf_op jit(solution)/shard_map/all_to_all | solution.py:558
  57.8 3.1 %collective-permute-start.7 = (bf16[3,64,128]{2,1,0:T(8,128)(2,1)S(1)}, bf16[3,64,128]{2,1,0:T(8,128)(2,1)S(1)}, u32[]{:S(2)}, u32[]{:S(2)}) collective-permute-start(bf16[3,64,128]{2,1,0:T(8,128)(2,1)S(1)} %get-tuple-element.71), channel_id=1, source_target_pairs={{4,8},{8,4},{12,16},{16,12},{20,24},{24,20},{5,9},{9,5},{13,17},{1... | collective-permute-start | bytes 147464 | tf_op jit(solution)/shard_map/ppermute | solution.py:472
  58.5 3.4 %collective-permute-start.6 = (bf16[3,64,128]{2,1,0:T(8,128)(2,1)S(1)}, bf16[3,64,128]{2,1,0:T(8,128)(2,1)S(1)}, u32[]{:S(2)}, u32[]{:S(2)}) collective-permute-start(bf16[3,64,128]{2,1,0:T(8,128)(2,1)S(1)} %get-tuple-element.72), channel_id=1, source_target_pairs={{0,4},{4,0},{8,12},{12,8},{16,20},{20,16},{24,28},{28,24},{1,5},{5... | collective-permute-start | bytes 147464 | tf_op jit(solution)/shard_map/ppermute | solution.py:473
  67.9 12.9 %all-to-all-start.3 = ((f32[32,9,128]{2,1,0:T(8,128)}), f32[32,9,128]{2,1,0:T(8,128)S(1)}, u32[]{:S(2)}, u32[]{:S(2)}) async-start(f32[32,9,128]{2,1,0:T(8,128)} %shard_map.110), calls=%async_computation.3 | async-start | bytes 524288 | tf_op jit(solution)/shard_map/all_to_all | solution.py:563
where the time goes:
time: 82.1 us; the launch traced here: 81.6 us
  Pallas kernels  22.7 us (28%)
  starting transfers between devices  19.3 us (24%)
  blocking collectives  19.1 us (23%)
  waiting for transfers between devices  15.9 us (19%)
  local copies, waits for them, and re-layouts  3.67 us (4%)
    pallas_call x9, Pallas kernels, call(): pl.pallas_call(kernel, out_shape=out_shape, in_specs=[pl.BlockSpec(memory...  17.8 us
    all_to_all x1, blocking collectives, on_device(): stats = lax.all_to_all(stat, axes, 0, 0)  10.2 us
    all_to_all x1, blocking collectives, on_device(): sums = lax.all_to_all(sums, axes, 0, 0)  8.88 us
    ppermute x2, starting transfers between devices, lon_swap(): second = lax.ppermute(side, 'lon', odd)  5.69 us
    ppermute x2, starting transfers between devices, lat_swap(): first = lax.ppermute(jnp.where(flag, up, dn), 'lat', even)  5.38 us
    all_to_all x1, waiting for transfers between devices, on_device(): wg = lax.all_to_all(shares, axes, 0, 0)  5.29 us
    all_to_all x1, waiting for transfers between devices, on_device(): parts = lax.all_to_all(wg, axes, 0, 0)  5.26 us
    pallas_call x2, Pallas kernels, backward(): pl.pallas_call(functools.partial(back_kernel, b), out_shape=S(state.shape...  4.92 us
  transfers between devices with their start and end apart: 10, of which 6 were waited for; matrix products, arithmetic and copies ran while one was open for 0% of the time, Pallas kernels for 9%

commit v1 on v0

--- a/solution.py
+++ b/solution.py
@@ -7,10 +7,10 @@
 from jax.experimental.pallas import tpu as pltpu
 from jax.sharding import PartitionSpec as P
 
+
 F32 = jnp.float32
 BF16 = jnp.bfloat16
 STEP = 2
-CHUNK = 16
 GROUP = 4
 EPS = 1e-05
 
@@ -30,53 +30,30 @@
     return hit
 
 
-def call(kernel, out_shape, scratch, flops, nbytes, *args, fetch=False):
-    space = pl.ANY if fetch else pltpu.VMEM
+def call(kernel, out_shape, scratch, flops, nbytes, *args):
     return pl.pallas_call(
         kernel,
         out_shape=out_shape,
-        in_specs=[pl.BlockSpec(memory_space=space)] * len(args),
+        in_specs=[pl.BlockSpec(memory_space=pltpu.VMEM)] * len(args),
         scratch_shapes=scratch,
         compiler_params=pltpu.CompilerParams(vmem_limit_bytes=24 << 20),
         cost_estimate=pl.CostEstimate(flops=flops, bytes_accessed=nbytes, transcendentals=0),
     )(*args)
 
 
-def flags(mask_ref):
-    return mask_ref[...].astype(F32)
-
-
 def row_lanes(h, width, count=1):
     return pl.ds(pl.multiple_of(h * width, width), count * width)
 
 
-def fetches(src_ref, buf, sems):
-    batch, chans = src_ref.shape[:2]
-    spots = [(b, c) for b in range(batch) for c in range(0, chans, CHUNK)]
-    copies = []
-    for n, (b, c) in enumerate(spots):
-        part = (b, pl.ds(c, CHUNK))
-        copies.append(pltpu.make_async_copy(src_ref.at[part], buf.at[part], sems.at[n]))
-    return spots, copies
-
-
-def spread_rows(src_ref, buf, sems, mask_ref, mbuf, msem, tmp):
-    batch, chans, high, width = src_ref.shape
-    head = pltpu.make_async_copy(mask_ref, mbuf, msem)
-    head.start()
-    spots, copies = fetches(src_ref, buf, sems)
-    for copy in copies:
-        copy.start()
-    head.wait()
-    mask = flags(mbuf)
-    for (b, c0), copy in zip(spots, copies):
-        copy.wait()
-        for c in range(c0, c0 + CHUNK):
+def spread_rows(src_ref, tmp, mask):
+    batch, chans, high, _ = src_ref.shape
+    for b in range(batch):
+        for c in range(chans):
             at = (b * chans + c) * (high + 1)
-            tmp[at : at + high, :] = buf[b, c].astype(F32) * mask
-
-
-def channel_rows(tmp, b, h, chans, high):
+            tmp[at : at + high, :] = src_ref[b, c].astype(F32) * mask
+
+
+def channel_rows(b, h, chans, high):
     return pl.ds(b * chans * (high + 1) + h, chans, stride=high + 1)
 
 
@@ -92,15 +69,16 @@
     return jnp.where(here, rolled(v, 2 * i, width), old)
 
 
-def gather_kernel(x_ref, mask_ref, xm_ref, top_ref, bot_ref, side_ref, tmp, buf, mbuf, sems, msem):
+def gather_kernel(x_ref, mask_ref, xm_ref, top_ref, bot_ref, side_ref, maskf, tmp):
     batch, chans, high, width = x_ref.shape
-    spread_rows(x_ref, buf, sems, mask_ref, mbuf, msem, tmp)
+    maskf[...] = mask_ref[...].astype(F32)
+    spread_rows(x_ref, tmp, maskf[...])
     lane = lane_of(chans, width)
     side = jnp.zeros((chans, width), F32)
     for b in range(batch):
 
         def row(h, side, b=b):
-            v = tmp[channel_rows(tmp, b, h, chans, high), :]
+            v = tmp[channel_rows(b, h, chans, high), :]
             xm_ref[b, :, row_lanes(h, width)] = v.astype(BF16)
             return packed(side, v, b * high + h, lane)
 
@@ -110,12 +88,9 @@
     side_ref[...] = side.astype(BF16)
 
 
-def relay_kernel(x_ref, mask_ref, w_hbm, out_ref, fwd_ref, back_ref, tmp, buf, mbuf, sems, msem, w_ref, wsem):
+def relay_kernel(x_ref, maskf, w_ref, out_ref, fwd_ref, back_ref, tmp):
     batch, chans, high, width = x_ref.shape
-    weights = pltpu.make_async_copy(w_hbm, w_ref, wsem)
-    weights.start()
-    spread_rows(x_ref, buf, sems, mask_ref, mbuf, msem, tmp)
-    weights.wait()
+    spread_rows(x_ref, tmp, maskf[...])
     for kx in range(3):
         part = jnp.concatenate([w_ref[ky, kx].astype(F32) for ky in range(3)], axis=0)
         fwd_ref[kx * chans : (kx + 1) * chans, :] = jnp.transpose(part).astype(BF16)
@@ -124,7 +99,7 @@
     for b in range(batch):
 
         def row(h, carry, b=b):
-            out_ref[b, :, row_lanes(h, width)] = tmp[channel_rows(tmp, b, h, chans, high), :].astype(BF16)
+            out_ref[b, :, row_lanes(h, width)] = tmp[channel_rows(b, h, chans, high), :].astype(BF16)
             return carry
 
         lax.fori_loop(0, high, row, 0, unroll=8)
@@ -225,13 +200,12 @@
 
 
 def conv_kernel(
-    x_ref, above_ref, below_ref, edge_ref, w_ref, mask_ref,
-    conv_ref, pad_ref, stack_ref, stat_ref, maskf, *bufs,
+    x_ref, above_ref, below_ref, edge_ref, w_ref, maskf,
+    conv_ref, pad_ref, stack_ref, stat_ref, *bufs,
 ):
-    batch, chans, flat = x_ref.shape
-    high, width = mask_ref.shape
+    batch, chans, _ = x_ref.shape
+    high, width = maskf.shape
     lane = lane_of(chans, width)
-    maskf[...] = flags(mask_ref)
     fill_padded(pad_ref, x_ref, above_ref, below_ref, width, range(batch))
     stack = edge_stack(edge_ref, above_ref, below_ref, high, batch)
     stack_ref[...] = stack
@@ -274,11 +248,10 @@
 
 
 def silu_kernel(
-    stat_ref, conv_ref, cot_ref, mask_ref, gain_ref, bias_ref, act_ref, dpre_ref, par_ref, sum_ref, maskf, tmp
+    stat_ref, conv_ref, cot_ref, maskf, gain_ref, bias_ref, act_ref, dpre_ref, par_ref, sum_ref, tmp
 ):
-    batch, chans, flat = conv_ref.shape
-    high, width = mask_ref.shape
-    maskf[...] = flags(mask_ref)
+    batch, chans, _ = conv_ref.shape
+    high, width = maskf.shape
     stat = stat_ref[:, 0, :]
     n = stat_ref[:, 1, :]
     count = jnp.maximum(jnp.sum(n, axis=0, keepdims=True), 1.0)
@@ -303,7 +276,7 @@
             t = jnp.tanh(half)
             s = 0.5 + 0.5 * t
             act = half + half * t
-            tmp[channel_rows(tmp, b, h, chans, high), :] = act * maskf[pl.ds(h, 1), :]
+            tmp[channel_rows(b, h, chans, high), :] = act * maskf[pl.ds(h, 1), :]
             dpre = cot_ref[b, :, at].astype(F32) * (s + act * (0.5 - 0.5 * t))
             dpre_ref[b, :, at] = dpre
             return sums[0] + dpre, sums[1] + dpre * dev
@@ -316,13 +289,12 @@
 
 
 def grad_kernel(
-    sum_ref, conv_ref, dpre_ref, par_ref, pad_ref, stack_ref, mask_ref,
-    d_ref, top_ref, bot_ref, side_ref, out_ref, bg_ref, gg_ref, maskf, acc, da, db, wg_ref,
+    sum_ref, conv_ref, dpre_ref, par_ref, pad_ref, stack_ref, maskf,
+    d_ref, top_ref, bot_ref, side_ref, out_ref, bg_ref, gg_ref, acc, da, db, wg_ref,
 ):
-    batch, chans, flat = conv_ref.shape
-    high, width = mask_ref.shape
+    batch, chans, _ = conv_ref.shape
+    high, width = maskf.shape
     lane = lane_of(chans, width)
-    maskf[...] = flags(mask_ref)
     both = jnp.sum(sum_ref[:, 0, :], axis=0, keepdims=True)
     bg_ref[...] = both[:, 0:chans]
     gg_ref[...] = both[:, chans : 2 * chans]
@@ -388,11 +360,12 @@
     wg_ref[3 * chans : 3 * chans + half, :] = jnp.concatenate(
         [full[0:half, 2 * chans :], full[half:, 2 * chans :]], axis=1
     )
-    share = out_ref.shape[1]
     if wg_ref.shape[0] > 3 * chans + half:
         wg_ref[3 * chans + half :, :] = jnp.zeros((wg_ref.shape[0] - 3 * chans - half, width), F32)
+    share = out_ref.shape[2] // width
     for p in range(out_ref.shape[0]):
-        out_ref[p] = wg_ref[p * share : (p + 1) * share, :]
+        for r in range(share):
+            out_ref[p, :, r * width : (r + 1) * width] = wg_ref[p * share + r : p * share + r + 1, :]
 
 
 def total_kernel(x_ref, out_ref):
@@ -402,9 +375,11 @@
 
 def unpack_kernel(chans, x_ref, out_ref, wg_ref):
     half = 3 * chans // 2
-    share = x_ref.shape[1]
+    width = wg_ref.shape[1]
+    share = x_ref.shape[2] // width
     for p in range(x_ref.shape[0]):
-        wg_ref[p * share : (p + 1) * share, :] = x_ref[p]
+        for r in range(share):
+            wg_ref[p * share + r : p * share + r + 1, :] = x_ref[p, :, r * width : (r + 1) * width]
     for ky in range(3):
         for kx in range(2):
             out_ref[ky, kx] = wg_ref[ky * chans : (ky + 1) * chans, kx * chans : (kx + 1) * chans]
@@ -419,17 +394,16 @@
         out_ref[ky, 2] = tail[ky * chans : (ky + 1) * chans]
 
 
-def back_kernel(plane, d_ref, above_ref, below_ref, edge_ref, w_ref, mask_ref, *rest):
-    out_ref, pad_ref, maskf, tmp, *bufs, tile, sem = rest[-10:]
-    batch, chans, flat = d_ref.shape
-    high, width = mask_ref.shape
+def back_kernel(plane, d_ref, above_ref, below_ref, edge_ref, w_ref, maskf, *rest):
+    out_ref, pad_ref, tmp, *bufs, tile, sem = rest[-9:]
+    batch, chans, _ = d_ref.shape
+    high, width = maskf.shape
     lane = lane_of(chans, width)
-    maskf[...] = flags(mask_ref)
     fill_padded(pad_ref, d_ref, above_ref, below_ref, width, [plane])
     fix = edge_fix(w_ref, edge_stack(edge_ref, above_ref, below_ref, high, batch), lane)
 
     def post(b, h, value, carry):
-        tmp[channel_rows(tmp, 0, h, chans, high), :] = value * maskf[pl.ds(h, 1), :]
+        tmp[channel_rows(0, h, chans, high), :] = value * maskf[pl.ds(h, 1), :]
         return carry
 
     conv_loop(pad_ref, w_ref, bufs, fix, plane, high, lane, post, 0)
@@ -493,29 +467,21 @@
     mat = 2 * batch * flat * 9 * chans * chans
     size = batch * chans * flat * 2
     tmp = pltpu.VMEM((batch * chans * (high + 1), width), F32)
-    maskf = pltpu.VMEM((high, width), F32)
     products = [pltpu.VMEM((3 * chans, STEP * width), F32)] * 4
     plane = S((batch, chans, flat), BF16)
     wide = S((batch, chans, flat), F32)
     rows = S((batch, chans, width), BF16)
     cols = S((chans, width), BF16)
     square = S((3 * chans, 3 * chans), BF16)
-    incoming = [
-        tmp,
-        pltpu.VMEM(state.shape, BF16),
-        pltpu.VMEM(land_mask.shape, jnp.int32),
-        pltpu.SemaphoreType.DMA((batch * chans // CHUNK,)),
-        pltpu.SemaphoreType.DMA,
-    ]
-    weights = [pltpu.VMEM(conv_weight.shape, BF16), pltpu.SemaphoreType.DMA]
-    xm, top, bot, side = call(
-        gather_kernel, (plane, rows, rows, cols), incoming, 0, 2 * size, state, land_mask, fetch=True
+    xm, top, bot, side, flag = call(
+        gather_kernel, (plane, rows, rows, cols, S((high, width), F32)), [tmp], 0, 2 * size, state, land_mask
     )
     cot, w_fwd, w_back = call(
-        relay_kernel, (plane, square, square), incoming + weights, 0, 2 * size,
-        cotangent, land_mask, conv_weight, fetch=True,
-    )
-    edge, up, dn = with_corners(top, bot, lon_swap(side), high)
+        relay_kernel, (plane, square, square), [tmp], 0, 2 * size, cotangent, flag, conv_weight
+    )
+    sides = lon_swap(side)
+    sides, cot, w_fwd, w_back = lax.optimization_barrier((sides, cot, w_fwd, w_back))
+    edge, up, dn = with_corners(top, bot, sides, high)
     above, below = lat_swap(up, dn)
     conv, padded, stack, stat = call(
         conv_kernel,
@@ -525,19 +491,19 @@
             S((3 * chans, width), BF16),
             S((devices, 2, 2 * chans), F32),
         ),
-        [maskf] + products,
+        products,
         4 * mat,
         4 * size,
-        xm, above, below, edge, w_fwd, land_mask,
+        xm, above, below, edge, w_fwd, flag,
     )
     stats = lax.all_to_all(stat, axes, 0, 0)
     activated, dpre, par, sums = call(
         silu_kernel,
         (S(state.shape, BF16), wide, S((chans, width), F32), S((devices, 1, 2 * chans), F32)),
-        [maskf, tmp],
+        [tmp],
         20 * size,
         6 * size,
-        stats, conv, cot, land_mask, norm_gain[None], batchnorm_bias[None],
+        stats, conv, cot, flag, norm_gain[None], batchnorm_bias[None],
     )
     sums = lax.all_to_all(sums, axes, 0, 0)
     stacked = pltpu.VMEM((3 * chans, GROUP * width), BF16)
@@ -547,19 +513,19 @@
         grad_kernel,
         (
             plane, rows, rows, cols,
-            S((devices, share, width), F32), S((1, chans), F32), S((1, chans), F32),
+            S((devices, 1, share * width), F32), S((1, chans), F32), S((1, chans), F32),
         ),
-        [maskf, pltpu.VMEM((3 * chans, 3 * chans), F32), stacked, stacked, flatg],
+        [pltpu.VMEM((3 * chans, 3 * chans), F32), stacked, stacked, flatg],
         4 * mat,
         6 * size,
-        sums, conv, dpre, par, padded, stack, land_mask,
+        sums, conv, dpre, par, padded, stack, flag,
     )
 
     parts = lax.all_to_all(wg, axes, 0, 0)
     edge, up, dn = with_corners(top, bot, lon_swap(side), high)
     above, below = lat_swap(up, dn)
     parts, above, below, edge = lax.optimization_barrier((parts, above, below, edge))
-    shares = call(total_kernel, S((devices, share, width), F32), [], 0, 600_000, parts)
+    shares = call(total_kernel, S((devices, 1, share * width), F32), [], 0, 600_000, parts)
     wg = lax.all_to_all(shares, axes, 0, 0)
 
     def backward(b, earlier):
@@ -574,7 +540,6 @@
             out_specs=far,
             scratch_shapes=[
                 pltpu.VMEM((1, chans, flat + 2 * width), BF16),
-                maskf,
                 pltpu.VMEM((chans * (high + 1), width), F32),
             ]
             + products
@@ -582,7 +547,7 @@
             compiler_params=pltpu.CompilerParams(vmem_limit_bytes=24 << 20),
             cost_estimate=pl.CostEstimate(flops=2 * mat, bytes_accessed=2 * size, transcendentals=0),
             **kept,
-        )(dmap, above, below, edge, w_back, land_mask, *extra)
+        )(dmap, above, below, edge, w_back, flag, *extra)
 
     state_grad = None
     for b in range(batch):

time: 82.1 us -> 76.6 us (0.933)
  waiting for transfers between devices: 15.9 us -> 10.9 us
  Pallas kernels: 22.7 us -> 19.6 us
  blocking collectives: 19.1 us -> 21 us
    pallas_call x9, Pallas kernels: 17.8 us -> 14.6 us  [call(): pl.pallas_call(kernel, out_shape=out_shape, in_specs=[pl.BlockSpec(memory...]
    all_to_all x1, blocking collectives: 10.2 us -> 12.1 us  [on_device(): stats = lax.all_to_all(stat, axes, 0, 0)]
    ppermute x2, waiting for transfers between devices: 2.46 us -> 0.75 us  [lon_swap(): second = lax.ppermute(side, 'lon', odd)]
    all_to_all x1, waiting for transfers between devices: 5.29 us -> 3.65 us  [on_device(): wg = lax.all_to_all(shares, axes, 0, 0)]
    all_to_all x1, waiting for transfers between devices: 5.26 us -> 3.64 us  [on_device(): parts = lax.all_to_all(wg, axes, 0, 0)]
    ppermute x2, waiting for transfers between devices: 2.02 us -> 1.13 us  [lon_swap(): first = lax.ppermute(side, 'lon', even)]
    ppermute x2, waiting for transfers between devices: 0.88 us -> 1.76 us  [lat_swap(): first = lax.ppermute(jnp.where(flag, up, dn), 'lat', even)]
    unnamed x16 -> x12, local copies, waits for them, and re-layouts: 3.67 us -> 4.08 us
  transfers between devices with their start and end apart: 10 -> 10, of which waited for: 6 -> 6; matrix products, arithmetic and copies ran while one was open for 0% -> 0% of each run, Pallas kernels for 9% -> 7%
where the time goes in v1:
time: 76.6 us; the launch traced here: 76.2 us
  blocking collectives  21 us (27%)
  starting transfers between devices  19.8 us (26%)
  Pallas kernels  19.6 us (26%)
  waiting for transfers between devices  10.9 us (14%)
  local copies, waits for them, and re-layouts  4.08 us (5%)
  between operations  0.77 us (1%)
    pallas_call x9, Pallas kernels, call(): pl.pallas_call(kernel, out_shape=out_shape, in_specs=[pl.BlockSpec(memory...  14.6 us
    all_to_all x1, blocking collectives, on_device(): stats = lax.all_to_all(stat, axes, 0, 0)  12.1 us
    all_to_all x1, blocking collectives, on_device(): sums = lax.all_to_all(sums, axes, 0, 0)  8.88 us
    ppermute x2, starting transfers between devices, lon_swap(): second = lax.ppermute(side, 'lon', odd)  5.7 us
    ppermute x2, starting transfers between devices, lat_swap(): first = lax.ppermute(jnp.where(flag, up, dn), 'lat', even)  5.38 us
    pallas_call x2, Pallas kernels, backward(): pl.pallas_call(functools.partial(back_kernel, b), out_shape=S(state.shape...  4.94 us
    unnamed x12, local copies, waits for them, and re-layouts  4.08 us
    all_to_all x1, starting transfers between devices, on_device(): parts = lax.all_to_all(wg, axes, 0, 0)  3.68 us
  transfers between devices with their start and end apart: 10, of which 6 were waited for; matrix products, arithmetic and copies ran while one was open for 0% of the time, Pallas kernels for 7%

profile of v1, /device:TPU:0, one launch (start us, length us, event | category | flops | bytes accessed | tf_op | source)
XLA Modules:
  0.0 76.2 jit_solution(7232684397536258767)
XLA Ops:
  0.6 0.0 copy-start.1
  0.6 1.2 %copy-done.1 = bf16[2,64,32,128]{3,2,1,0:T(8,128)(2,1)S(1)} copy-done((bf16[2,64,32,128]{3,2,1,0:T(8,128)(2,1)S(1)}, bf16[2,64,32,128]{3,2,1,0:T(8,128)(2,1)}, u32[]{:S(2)}) %copy-start.1) | copy-done | bytes 1048600
  1.9 0.0 copy-start.3
  1.9 0.7 copy-done.3
  2.6 1.3 %shard_map.101 = (bf16[2,64,4096]{2,1,0:T(8,128)(2,1)S(1)}, bf16[2,64,128]{2,1,0:T(8,128)(2,1)S(1)}, bf16[2,64,128]{2,1,0:T(8,128)(2,1)S(1)}, bf16[64,128]{1,0:T(8,128)(2,1)S(1)}, f32[32,128]{1,0:T(8,128)S(1)}) custom-call(bf16[2,64,32,128]{3,2,1,0:T(8,128)(2,1)S(1)} %copy-done.1, s32[32,128]{1,0:T(8,128)S(1)} %copy-done.3), custom_call_target="tpu_custom_call" | custom-call | bytes 2097152 | tf_op jit(solution)/shard_map/pallas_call | solution.py:34
  3.9 5.1 %collective-permute-start.1 = (bf16[64,128]{1,0:T(8,128)(2,1)S(1)}, bf16[64,128]{1,0:T(8,128)(2,1)S(1)}, u32[]{:S(2)}, u32[]{:S(2)}) collective-permute-start(bf16[64,128]{1,0:T(8,128)(2,1)S(1)} %get-tuple-element.46), channel_id=1, source_target_pairs={{0,3},{1,2},{2,1},{3,0},{4,7},{5,6},{6,5},{7,4},{8,11},{9,10},{10,... | collective-permute-start | bytes 49160 | tf_op jit(solution)/shard_map/ppermute | solution.py:433
  9.1 0.0 collective-permute-start
  9.1 0.0 copy-start
  9.1 1.2 %copy-done = bf16[2,64,32,128]{3,2,1,0:T(8,128)(2,1)S(1)} copy-done((bf16[2,64,32,128]{3,2,1,0:T(8,128)(2,1)S(1)}, bf16[2,64,32,128]{3,2,1,0:T(8,128)(2,1)}, u32[]{:S(2)}) %copy-start) | copy-done | bytes 1048600
  10.3 0.0 copy-start.2
  10.3 0.9 %copy-done.2 = bf16[3,3,64,64]{3,2,1,0:T(8,128)(2,1)S(1)} copy-done((bf16[3,3,64,64]{3,2,1,0:T(8,128)(2,1)S(1)}, bf16[3,3,64,64]{3,2,1,0:T(8,128)(2,1)}, u32[]{:S(2)}) %copy-start.2) | copy-done | bytes 73752
  11.2 0.5 shard_map.102
  11.7 0.0 collective-permute-done.1
  11.7 1.1 %collective-permute-done = bf16[64,128]{1,0:T(8,128)(2,1)S(1)} collective-permute-done((bf16[64,128]{1,0:T(8,128)(2,1)S(1)}, bf16[64,128]{1,0:T(8,128)(2,1)S(1)}, u32[]{:S(2)}, u32[]{:S(2)}) %collective-permute-start) | collective-permute-done | bytes 16416 | tf_op jit(solution)/shard_map/ppermute | solution.py:432
  12.8 0.2 shard_map.103
  13.0 0.7 collective-permute-start.3
  13.7 2.9 %collective-permute-start.2 = (bf16[3,64,128]{2,1,0:T(8,128)(2,1)S(1)}, bf16[3,64,128]{2,1,0:T(8,128)(2,1)S(1)}, u32[]{:S(2)}, u32[]{:S(2)}) collective-permute-start(bf16[3,64,128]{2,1,0:T(8,128)(2,1)S(1)} %get-tuple-element.88), channel_id=1, source_target_pairs={{0,4},{4,0},{8,12},{12,8},{16,20},{20,16},{24,28},{28,24},{1,5},{5... | collective-permute-start | bytes 147464 | tf_op jit(solution)/shard_map/ppermute | solution.py:447
  16.6 0.0 collective-permute-done.3
  16.6 0.9 %collective-permute-done.2 = bf16[3,64,128]{2,1,0:T(8,128)(2,1)S(1)} collective-permute-done((bf16[3,64,128]{2,1,0:T(8,128)(2,1)S(1)}, bf16[3,64,128]{2,1,0:T(8,128)(2,1)S(1)}, u32[]{:S(2)}, u32[]{:S(2)}) %collective-permute-start.2) | collective-permute-done | bytes 49184 | tf_op jit(solution)/shard_map/ppermute | solution.py:447
  17.5 0.0 copy-start.4
  17.5 0.0 copy-start.5
  17.5 3.5 %shard_map.104 = (f32[2,64,4096]{2,1,0:T(8,128)S(1)}, bf16[2,64,4352]{2,1,0:T(8,128)(2,1)S(1)}, bf16[192,128]{1,0:T(8,128)(2,1)S(1)}, f32[32,2,128]{2,1,0:T(2,128)S(1)}) custom-call(bf16[2,64,4096]{2,1,0:T(8,128)(2,1)S(1)} %get-tuple-element.43.x_ref, bf16[3,64,128]{2,1,0:T(8,128)(2,1)S(1)} %get-tuple-element.86.above_ref, ...), custom_call_target="tpu_custom_call" | custom-call | flops 2415919104 | bytes 4194304 | tf_op jit(solution)/shard_map/pallas_call | solution.py:34
  21.0 12.1 %all_to_all.20.stat_ref = f32[32,2,128]{2,1,0:T(2,128)S(1)} all-to-all(f32[32,2,128]{2,1,0:T(2,128)S(1)} %get-tuple-element.57), channel_id=1, replica_groups=mesh['lat'=8,'lon'=4] {'lat','lon'}, dimensions={0} | all-to-all | bytes 65536 | tf_op jit(solution)/shard_map/all_to_all | solution.py:499
  33.1 0.0 copy-done.4
  33.1 0.0 copy-done.5
  33.1 2.9 %shard_map.105 = (bf16[2,64,32,128]{3,2,1,0:T(8,128)(2,1)}, f32[2,64,4096]{2,1,0:T(8,128)S(1)}, f32[64,128]{1,0:T(8,128)S(1)}, f32[32,1,128]{2,1,0:T(1,128)S(1)}) custom-call(f32[32,2,128]{2,1,0:T(2,128)S(1)} %all_to_all.20.stat_ref, f32[2,64,4096]{2,1,0:T(8,128)S(1)} %get-tuple-element.58.conv_ref, bf16[2,64,4096]{2,1,0:T(8,128)(2,1)S(1)} %get-tuple-element.59.cot_ref, ...), custom_call_target="tpu_custom_call" | custom-call | flops 20971520 | bytes 6291456 | tf_op jit(solution)/shard_map/pallas_call | solution.py:34
  36.0 8.9 %all_to_all.21.sum_ref = f32[32,1,128]{2,1,0:T(1,128)S(1)} all-to-all(f32[32,1,128]{2,1,0:T(1,128)S(1)} %get-tuple-element.61), channel_id=1, replica_groups=mesh['lat'=8,'lon'=4] {'lat','lon'}, dimensions={0} | all-to-all | bytes 32768 | tf_op jit(solution)/shard_map/all_to_all | solution.py:508
  44.9 4.5 %shard_map.106 = (bf16[2,64,4096]{2,1,0:T(8,128)(2,1)S(1)}, bf16[2,64,128]{2,1,0:T(8,128)(2,1)S(1)}, bf16[2,64,128]{2,1,0:T(8,128)(2,1)S(1)}, bf16[64,128]{1,0:T...) custom-call(f32[32,1,128]{2,1,0:T(1,128)S(1)} %all_to_all.21.sum_ref, ...), custom_call_target="tpu_custom_call" | custom-call | flops 2415919104 | bytes 6291456 | tf_op jit(solution)/shard_map/pallas_call | solution.py:34
  49.4 0.6 collective-permute-start.5
  50.0 0.5 collective-permute-start.4
  50.5 3.7 %all-to-all-start.2 = ((f32[32,1,1152]{2,1,0:T(1,128)}), f32[32,1,1152]{2,1,0:T(1,128)S(1)}, u32[]{:S(2)}, u32[]{:S(2)}) async-start(f32[32,1,1152]{2,1,0:T(1,128)} %get-tuple-element.67), calls=%async_computation.2 | async-start | bytes 294912 | tf_op jit(solution)/shard_map/all_to_all | solution.py:524
  54.2 0.7 collective-permute-done.5
  55.0 0.0 collective-permute-done.4
  55.0 0.2 shard_map.107
  55.2 0.7 collective-permute-start.7
  55.8 2.5 %collective-permute-start.6 = (bf16[3,64,128]{2,1,0:T(8,128)(2,1)S(1)}, bf16[3,64,128]{2,1,0:T(8,128)(2,1)S(1)}, u32[]{:S(2)}, u32[]{:S(2)}) collective-permute-start(bf16[3,64,128]{2,1,0:T(8,128)(2,1)S(1)} %get-tuple-element.84), channel_id=1, source_target_pairs={{0,4},{4,0},{8,12},{12,8},{16,20},{20,16},{24,28},{28,24},{1,5},{5... | collective-permute-start | bytes 147464 | tf_op jit(solution)/shard_map/ppermute | solution.py:447
  58.3 0.0 collective-permute-done.7
  58.3 0.9 %collective-permute-done.6 = bf16[3,64,128]{2,1,0:T(8,128)(2,1)S(1)} collective-permute-done((bf16[3,64,128]{2,1,0:T(8,128)(2,1)S(1)}, bf16[3,64,128]{2,1,0:T(8,128)(2,1)S(1)}, u32[]{:S(2)}, u32[]{:S(2)}) %collective-permute-start.6) | collective-permute-done | bytes 49184 | tf_op jit(solution)/shard_map/ppermute | solution.py:447
  59.2 3.6 %all-to-all-done.2.x_ref = f32[32,1,1152]{2,1,0:T(1,128)S(1)} async-done(((f32[32,1,1152]{2,1,0:T(1,128)}), f32[32,1,1152]{2,1,0:T(1,128)S(1)}, u32[]{:S(2)}, u32[]{:S(2)}) %all-to-all-start.2) | async-done | bytes 147488 | tf_op jit(solution)/shard_map/all_to_all | solution.py:524
  62.8 0.8 %shard_map.110 = f32[32,1,1152]{2,1,0:T(1,128)} custom-call(f32[32,1,1152]{2,1,0:T(1,128)S(1)} %all-to-all-done.2.x_ref), custom_call_target="tpu_custom_call" | custom-call | bytes 600000 | tf_op jit(solution)/shard_map/pallas_call | solution.py:34
  63.6 3.1 %all-to-all-start.3 = ((f32[32,1,1152]{2,1,0:T(1,128)}), f32[32,1,1152]{2,1,0:T(1,128)S(1)}, u32[]{:S(2)}, u32[]{:S(2)}) async-start(f32[32,1,1152]{2,1,0:T(1,128)} %shard_map.110), calls=%async_computation.3 | async-start | bytes 294912 | tf_op jit(solution)/shard_map/all_to_all | solution.py:529
  66.7 2.5 %shard_map.108.rest_0_ = bf16[2,64,32,128]{3,2,1,0:T(8,128)(2,1)} custom-call(bf16[2,64,4096]{2,1,0:T(8,128)(2,1)S(1)} %get-tuple-element.66.d_ref, bf16[3,64,128]{2,1,0:T(8,128)(2,1)S(1)} %get-tuple-element.74.above_ref, bf16[3,64,128]{2,1,0:T(8,128)(2,1)S(1)} %get-tuple-element.75.below_ref, bf16[64,128]{1,0:T(8,128)(2,1)S(1)} %get-tuple-element.76.edge_ref, ...), custom_call_target="tpu_custom_call" | custom-call | flops 1207959552 | bytes 2097152 | tf_op jit(solution)/shard_map/pallas_call | solution.py:536
  69.2 2.5 %shard_map.109 = bf16[2,64,32,128]{3,2,1,0:T(8,128)(2,1)} custom-call(bf16[2,64,4096]{2,1,0:T(8,128)(2,1)S(1)} %get-tuple-element.66.d_ref, bf16[3,64,128]{2,1,0:T(8,128)(2,1)S(1)} %get-tuple-element.74.above_ref, bf16[3,64,128]{2,1,0:T(8,128)(2,1)S(1)} %get-tuple-element.75.below_ref, ...), custom_call_target="tpu_custom_call", output_to_operand_aliasing={{}: (6, {})} | custom-call | flops 1207959552 | bytes 2097152 | tf_op jit(solution)/shard_map/pallas_call | solution.py:536
  71.7 3.7 %all-to-all-done.3.x_ref = f32[32,1,1152]{2,1,0:T(1,128)S(1)} async-done(((f32[32,1,1152]{2,1,0:T(1,128)}), f32[32,1,1152]{2,1,0:T(1,128)S(1)}, u32[]{:S(2)}, u32[]{:S(2)}) %all-to-all-start.3) | async-done | bytes 147488 | tf_op jit(solution)/shard_map/all_to_all | solution.py:529
  75.3 0.8 %shard_map.111 = f32[3,3,64,64]{3,2,1,0:T(8,128)} custom-call(f32[32,1,1152]{2,1,0:T(1,128)S(1)} %all-to-all-done.3.x_ref), custom_call_target="tpu_custom_call" | custom-call | bytes 500000 | tf_op jit(solution)/shard_map/pallas_call | solution.py:34
  (6 shorter events, 0.1 us)
Async XLA Ops:
  0.6 1.2 %copy-start.1 = (bf16[2,64,32,128]{3,2,1,0:T(8,128)(2,1)S(1)}, bf16[2,64,32,128]{3,2,1,0:T(8,128)(2,1)}, u32[]{:S(2)}) copy-start(bf16[2,64,32,128]{3,2,1,0:T(8,128)(2,1)} %x_ref.2) | copy-start | bytes 3145732
  1.9 0.7 copy-start.3
  3.9 7.8 %collective-permute-start.1 = (bf16[64,128]{1,0:T(8,128)(2,1)S(1)}, bf16[64,128]{1,0:T(8,128)(2,1)S(1)}, u32[]{:S(2)}, u32[]{:S(2)}) collective-permute-start(bf16[64,128]{1,0:T(8,128)(2,1)S(1)} %get-tuple-element.46), channel_id=1, source_target_pairs={{0,3},{1,2},{2,1},{3,0},{4,7},{5,6},{6,5},{7,4},{8,11},{9,10},{10,... | collective-permute-start | bytes 49160 | tf_op jit(solution)/shard_map/ppermute | solution.py:433
  9.1 3.7 %collective-permute-start = (bf16[64,128]{1,0:T(8,128)(2,1)S(1)}, bf16[64,128]{1,0:T(8,128)(2,1)S(1)}, u32[]{:S(2)}, u32[]{:S(2)}) collective-permute-start(bf16[64,128]{1,0:T(8,128)(2,1)S(1)} %get-tuple-element.46), channel_id=1, source_target_pairs={{0,1},{1,0},{2,3},{3,2},{4,5},{5,4},{6,7},{7,6},{8,9},{9,8},{10,11... | collective-permute-start | bytes 49160 | tf_op jit(solution)/shard_map/ppermute | solution.py:432
  9.1 1.2 %copy-start = (bf16[2,64,32,128]{3,2,1,0:T(8,128)(2,1)S(1)}, bf16[2,64,32,128]{3,2,1,0:T(8,128)(2,1)}, u32[]{:S(2)}) copy-start(bf16[2,64,32,128]{3,2,1,0:T(8,128)(2,1)} %x_ref.3) | copy-start | bytes 3145732
  10.3 0.9 %copy-start.2 = (bf16[3,3,64,64]{3,2,1,0:T(8,128)(2,1)S(1)}, bf16[3,3,64,64]{3,2,1,0:T(8,128)(2,1)}, u32[]{:S(2)}) copy-start(bf16[3,3,64,64]{3,2,1,0:T(8,128)(2,1)} %w_ref.1) | copy-start | bytes 221188
  13.0 3.6 %collective-permute-start.3 = (bf16[3,64,128]{2,1,0:T(8,128)(2,1)S(1)}, bf16[3,64,128]{2,1,0:T(8,128)(2,1)S(1)}, u32[]{:S(2)}, u32[]{:S(2)}) collective-permute-start(bf16[3,64,128]{2,1,0:T(8,128)(2,1)S(1)} %get-tuple-element.87), channel_id=1, source_target_pairs={{4,8},{8,4},{12,16},{16,12},{20,24},{24,20},{5,9},{9,5},{13,17},{1... | collective-permute-start | bytes 147464 | tf_op jit(solution)/shard_map/ppermute | solution.py:446
  13.7 3.8 %collective-permute-start.2 = (bf16[3,64,128]{2,1,0:T(8,128)(2,1)S(1)}, bf16[3,64,128]{2,1,0:T(8,128)(2,1)S(1)}, u32[]{:S(2)}, u32[]{:S(2)}) collective-permute-start(bf16[3,64,128]{2,1,0:T(8,128)(2,1)S(1)} %get-tuple-element.88), channel_id=1, source_target_pairs={{0,4},{4,0},{8,12},{12,8},{16,20},{20,16},{24,28},{28,24},{1,5},{5... | collective-permute-start | bytes 147464 | tf_op jit(solution)/shard_map/ppermute | solution.py:447
  17.5 15.6 %copy-start.4 = (f32[64]{0:T(128)S(1)}, f32[64]{0:T(128)}, u32[]{:S(2)}) copy-start(f32[64]{0:T(128)} %param.9) | copy-start | bytes 772
  17.5 15.6 %copy-start.5 = (f32[64]{0:T(128)S(1)}, f32[64]{0:T(128)}, u32[]{:S(2)}) copy-start(f32[64]{0:T(128)} %param.10) | copy-start | bytes 772
  49.4 5.5 %collective-permute-start.5 = (bf16[64,128]{1,0:T(8,128)(2,1)S(1)}, bf16[64,128]{1,0:T(8,128)(2,1)S(1)}, u32[]{:S(2)}, u32[]{:S(2)}) collective-permute-start(bf16[64,128]{1,0:T(8,128)(2,1)S(1)} %get-tuple-element.70), channel_id=1, source_target_pairs={{0,3},{1,2},{2,1},{3,0},{4,7},{5,6},{6,5},{7,4},{8,11},{9,10},{10,... | collective-permute-start | bytes 49160 | tf_op jit(solution)/shard_map/ppermute | solution.py:433
  50.0 5.0 %collective-permute-start.4 = (bf16[64,128]{1,0:T(8,128)(2,1)S(1)}, bf16[64,128]{1,0:T(8,128)(2,1)S(1)}, u32[]{:S(2)}, u32[]{:S(2)}) collective-permute-start(bf16[64,128]{1,0:T(8,128)(2,1)S(1)} %get-tuple-element.70), channel_id=1, source_target_pairs={{0,1},{1,0},{2,3},{3,2},{4,5},{5,4},{6,7},{7,6},{8,9},{9,8},{10,11... | collective-permute-start | bytes 49160 | tf_op jit(solution)/shard_map/ppermute | solution.py:432
  50.5 12.3 %all-to-all-start.2 = ((f32[32,1,1152]{2,1,0:T(1,128)}), f32[32,1,1152]{2,1,0:T(1,128)S(1)}, u32[]{:S(2)}, u32[]{:S(2)}) async-start(f32[32,1,1152]{2,1,0:T(1,128)} %get-tuple-element.67), calls=%async_computation.2 | async-start | bytes 294912 | tf_op jit(solution)/shard_map/all_to_all | solution.py:524
  55.2 3.1 %collective-permute-start.7 = (bf16[3,64,128]{2,1,0:T(8,128)(2,1)S(1)}, bf16[3,64,128]{2,1,0:T(8,128)(2,1)S(1)}, u32[]{:S(2)}, u32[]{:S(2)}) collective-permute-start(bf16[3,64,128]{2,1,0:T(8,128)(2,1)S(1)} %get-tuple-element.83), channel_id=1, source_target_pairs={{4,8},{8,4},{12,16},{16,12},{20,24},{24,20},{5,9},{9,5},{13,17},{1... | collective-permute-start | bytes 147464 | tf_op jit(solution)/shard_map/ppermute | solution.py:446
  55.8 3.4 %collective-permute-start.6 = (bf16[3,64,128]{2,1,0:T(8,128)(2,1)S(1)}, bf16[3,64,128]{2,1,0:T(8,128)(2,1)S(1)}, u32[]{:S(2)}, u32[]{:S(2)}) collective-permute-start(bf16[3,64,128]{2,1,0:T(8,128)(2,1)S(1)} %get-tuple-element.84), channel_id=1, source_target_pairs={{0,4},{4,0},{8,12},{12,8},{16,20},{20,16},{24,28},{28,24},{1,5},{5... | collective-permute-start | bytes 147464 | tf_op jit(solution)/shard_map/ppermute | solution.py:447
  63.6 11.7 %all-to-all-start.3 = ((f32[32,1,1152]{2,1,0:T(1,128)}), f32[32,1,1152]{2,1,0:T(1,128)S(1)}, u32[]{:S(2)}, u32[]{:S(2)}) async-start(f32[32,1,1152]{2,1,0:T(1,128)} %shard_map.110), calls=%async_computation.3 | async-start | bytes 294912 | tf_op jit(solution)/shard_map/all_to_all | solution.py:529

commit v2 on v1

--- a/solution.py
+++ b/solution.py
@@ -69,9 +69,20 @@
     return jnp.where(here, rolled(v, 2 * i, width), old)
 
 
-def gather_kernel(x_ref, mask_ref, xm_ref, top_ref, bot_ref, side_ref, maskf, tmp):
+def ends_kernel(x_ref, mask_ref, top_ref, bot_ref, maskf, tmp):
+    batch, chans, high, _ = x_ref.shape
+    maskf[...] = mask_ref[...].astype(F32)
+    for h, out_ref in ((0, top_ref), (high - 1, bot_ref)):
+        base = h - h % 16
+        for b in range(batch):
+            for c in range(chans):
+                tile = x_ref[b, c, base : base + 16].astype(F32)
+                tmp[c : c + 1, :] = tile[h - base : h - base + 1]
+            out_ref[b] = (tmp[...] * maskf[h : h + 1, :]).astype(BF16)
+
+
+def gather_kernel(x_ref, maskf, xm_ref, side_ref, tmp):
     batch, chans, high, width = x_ref.shape
-    maskf[...] = mask_ref[...].astype(F32)
     spread_rows(x_ref, tmp, maskf[...])
     lane = lane_of(chans, width)
     side = jnp.zeros((chans, width), F32)
@@ -83,8 +94,6 @@
             return packed(side, v, b * high + h, lane)
 
         side = lax.fori_loop(0, high, row, side, unroll=8)
-        top_ref[b] = xm_ref[b, :, 0:width]
-        bot_ref[b] = xm_ref[b, :, (high - 1) * width : high * width]
     side_ref[...] = side.astype(BF16)
 
 
@@ -110,7 +119,18 @@
     return first, [(p + 2 * (high - 1)) % width for p in first]
 
 
-def corner_kernel(high, batch, top_ref, bot_ref, fl_ref, fr_ref, edge_ref, up_ref, dn_ref):
+def corner_kernel(high, side_ref, above_ref, below_ref, out_ref):
+    chans, width = side_ref.shape
+    lane = lane_of(chans, width)
+    pack = jnp.zeros((chans, width), F32)
+    for b in range(above_ref.shape[0]):
+        pack = packed(pack, above_ref[b].astype(F32), b * high, lane)
+        pack = packed(pack, below_ref[b].astype(F32), b * high + high - 1, lane)
+    out_ref[0] = side_ref[...]
+    out_ref[1] = pack.astype(BF16)
+
+
+def pole_kernel(high, batch, top_ref, bot_ref, fl_ref, fr_ref, edge_ref, up_ref, dn_ref):
     chans, width = fl_ref.shape
     lane = lane_of(chans, width)
     even = lax.rem(lane, 2) == 0
@@ -129,13 +149,18 @@
     dn_ref[batch] = dn.astype(BF16)
 
 
-def edge_stack(edge_ref, above_ref, below_ref, high, batch):
-    chans, width = edge_ref.shape
+def facing(left, right):
+    chans, width = left.shape
+    even = lax.rem(lane_of(chans, width), 2) == 0
+    return jnp.where(even, rolled(left.astype(F32), 1, width), rolled(right.astype(F32), -1, width))
+
+
+def edge_stack(edge, above, below, high, batch):
+    chans, width = edge.shape
     lane = lane_of(chans, width)
-    edge = edge_ref[...].astype(F32)
     first, last = corners(high, batch, width)
-    top = jnp.where(any_lane(lane, first), above_ref[batch].astype(F32), rolled(edge, 2, width))
-    bottom = jnp.where(any_lane(lane, last), below_ref[batch].astype(F32), rolled(edge, -2, width))
+    top = jnp.where(any_lane(lane, first), above.astype(F32), rolled(edge, 2, width))
+    bottom = jnp.where(any_lane(lane, last), below.astype(F32), rolled(edge, -2, width))
     return jnp.concatenate([top, edge, bottom], axis=0).astype(BF16)
 
 
@@ -200,14 +225,15 @@
 
 
 def conv_kernel(
-    x_ref, above_ref, below_ref, edge_ref, w_ref, maskf,
+    x_ref, above_ref, below_ref, left_ref, right_ref, w_ref, maskf,
     conv_ref, pad_ref, stack_ref, stat_ref, *bufs,
 ):
     batch, chans, _ = x_ref.shape
     high, width = maskf.shape
     lane = lane_of(chans, width)
     fill_padded(pad_ref, x_ref, above_ref, below_ref, width, range(batch))
-    stack = edge_stack(edge_ref, above_ref, below_ref, high, batch)
+    corner = facing(left_ref[1], right_ref[1])
+    stack = edge_stack(facing(left_ref[0], right_ref[0]), corner, corner, high, batch)
     stack_ref[...] = stack
     fix = edge_fix(w_ref, stack, lane)
 
@@ -290,7 +316,7 @@
 
 def grad_kernel(
     sum_ref, conv_ref, dpre_ref, par_ref, pad_ref, stack_ref, maskf,
-    d_ref, top_ref, bot_ref, side_ref, out_ref, bg_ref, gg_ref, acc, da, db, wg_ref,
+    d_ref, top_ref, bot_ref, side_ref, out_ref, bg_ref, gg_ref, acc, wg_ref, *bufs,
 ):
     batch, chans, _ = conv_ref.shape
     high, width = maskf.shape
@@ -330,21 +356,25 @@
 
     def product(k, buf):
         b, j = place(k)
-        rhs = buf[...]
-        return lax.dot_general(taps(pad_ref, b, j, width, GROUP), rhs, contract, preferred_element_type=F32)
-
-    def pair(p, side):
-        k = 2 * p
-        gain = product(k, da)
-        side = build(k + 1, db, side)
+        return lax.dot_general(
+            taps(pad_ref, b, j, width, GROUP), buf[...], contract, preferred_element_type=F32
+        )
+
+    def four(p, side):
+        k = 4 * p
+        gain = product(k, bufs[0]) + product(k + 1, bufs[1])
+        side = build(k + 2, bufs[2], side)
+        side = build(k + 3, bufs[3], side)
         acc[...] += gain
-        gain = product(k + 1, db)
-        side = build(jnp.minimum(k + 2, steps - 1), da, side)
+        gain = product(k + 2, bufs[2]) + product(k + 3, bufs[3])
+        side = build(jnp.minimum(k + 4, steps - 1), bufs[0], side)
+        side = build(jnp.minimum(k + 5, steps - 1), bufs[1], side)
         acc[...] += gain
         return side
 
-    side = build(0, da, jnp.zeros((chans, width), F32))
-    side = lax.fori_loop(0, steps // 2, pair, side)
+    side = build(0, bufs[0], jnp.zeros((chans, width), F32))
+    side = build(1, bufs[1], side)
+    side = lax.fori_loop(0, steps // 4, four, side)
     for b in range(batch):
         top_ref[b] = d_ref[b, :, 0:width]
         bot_ref[b] = d_ref[b, :, (high - 1) * width : high * width]
@@ -366,11 +396,6 @@
     for p in range(out_ref.shape[0]):
         for r in range(share):
             out_ref[p, :, r * width : (r + 1) * width] = wg_ref[p * share + r : p * share + r + 1, :]
-
-
-def total_kernel(x_ref, out_ref):
-    total = jnp.sum(x_ref[...], axis=0, keepdims=True)
-    out_ref[...] = jnp.broadcast_to(total, out_ref.shape)
 
 
 def unpack_kernel(chans, x_ref, out_ref, wg_ref):
@@ -400,7 +425,8 @@
     high, width = maskf.shape
     lane = lane_of(chans, width)
     fill_padded(pad_ref, d_ref, above_ref, below_ref, width, [plane])
-    fix = edge_fix(w_ref, edge_stack(edge_ref, above_ref, below_ref, high, batch), lane)
+    stack = edge_stack(edge_ref[...].astype(F32), above_ref[batch], below_ref[batch], high, batch)
+    fix = edge_fix(w_ref, stack, lane)
 
     def post(b, h, value, carry):
         tmp[channel_rows(0, h, chans, high), :] = value * maskf[pl.ds(h, 1), :]
@@ -448,14 +474,19 @@
     return jnp.where(flag, first, second), jnp.where(flag, second, first)
 
 
-def with_corners(top, bot, sides, high):
+def with_corners(side, above, below, high):
+    shape = jax.ShapeDtypeStruct((2,) + side.shape, BF16)
+    return call(functools.partial(corner_kernel, high), shape, [], 0, 200_000, side, above, below)
+
+
+def with_poles(top, bot, sides, high):
     batch, chans, width = top.shape
     shapes = (
         jax.ShapeDtypeStruct((chans, width), BF16),
         jax.ShapeDtypeStruct((batch + 1, chans, width), BF16),
         jax.ShapeDtypeStruct((batch + 1, chans, width), BF16),
     )
-    return call(functools.partial(corner_kernel, high, batch), shapes, [], 0, 200_000, top, bot, *sides)
+    return call(functools.partial(pole_kernel, high, batch), shapes, [], 0, 200_000, top, bot, *sides)
 
 
 def on_device(state, land_mask, conv_weight, norm_gain, batchnorm_bias, cotangent):
@@ -473,16 +504,16 @@
     rows = S((batch, chans, width), BF16)
     cols = S((chans, width), BF16)
     square = S((3 * chans, 3 * chans), BF16)
-    xm, top, bot, side, flag = call(
-        gather_kernel, (plane, rows, rows, cols, S((high, width), F32)), [tmp], 0, 2 * size, state, land_mask
-    )
+    top, bot, flag = call(
+        ends_kernel, (rows, rows, S((high, width), F32)), [pltpu.VMEM((chans, width), F32)], 0, size // 8,
+        state, land_mask,
+    )
+    above, below = lat_swap(top, bot)
+    xm, side = call(gather_kernel, (plane, cols), [tmp], 0, 2 * size, state, flag)
     cot, w_fwd, w_back = call(
         relay_kernel, (plane, square, square), [tmp], 0, 2 * size, cotangent, flag, conv_weight
     )
-    sides = lon_swap(side)
-    sides, cot, w_fwd, w_back = lax.optimization_barrier((sides, cot, w_fwd, w_back))
-    edge, up, dn = with_corners(top, bot, sides, high)
-    above, below = lat_swap(up, dn)
+    left, right = lon_swap(with_corners(side, above, below, high))
     conv, padded, stack, stat = call(
         conv_kernel,
         (
@@ -494,7 +525,7 @@
         products,
         4 * mat,
         4 * size,
-        xm, above, below, edge, w_fwd, flag,
+        xm, above, below, left, right, w_fwd, flag,
     )
     stats = lax.all_to_all(stat, axes, 0, 0)
     activated, dpre, par, sums = call(
@@ -515,17 +546,17 @@
             plane, rows, rows, cols,
             S((devices, 1, share * width), F32), S((1, chans), F32), S((1, chans), F32),
         ),
-        [pltpu.VMEM((3 * chans, 3 * chans), F32), stacked, stacked, flatg],
+        [pltpu.VMEM((3 * chans, 3 * chans), F32), flatg, stacked, stacked, stacked, stacked],
         4 * mat,
         6 * size,
         sums, conv, dpre, par, padded, stack, flag,
     )
 
     parts = lax.all_to_all(wg, axes, 0, 0)
-    edge, up, dn = with_corners(top, bot, lon_swap(side), high)
+    edge, up, dn = with_poles(top, bot, lon_swap(side), high)
     above, below = lat_swap(up, dn)
     parts, above, below, edge = lax.optimization_barrier((parts, above, below, edge))
-    shares = call(total_kernel, S((devices, 1, share * width), F32), [], 0, 600_000, parts)
+    shares = jnp.broadcast_to(jnp.sum(parts, axis=0, keepdims=True), parts.shape)
     wg = lax.all_to_all(shares, axes, 0, 0)
 
     def backward(b, earlier):

time: 76.6 us -> 75.1 us (0.980)
  Pallas kernels: 19.6 us -> 18.2 us
  waiting for transfers between devices: 10.9 us -> 12.3 us
  local copies, waits for them, and re-layouts: 4.08 us -> 2.69 us
    unnamed x12, local copies, waits for them, and re-layouts: 4.08 us -> 1.95 us
    ppermute x2, waiting for transfers between devices: 0.75 us -> 2.38 us  [lon_swap(): second = lax.ppermute(side, 'lon', odd)]
    ppermute x2, starting transfers between devices: 5.7 us -> 4.22 us  [lon_swap(): second = lax.ppermute(side, 'lon', odd)]
    ppermute x2, starting transfers between devices: 5.38 us -> 6.86 us  [lat_swap(): first = lax.ppermute(jnp.where(flag, up, dn), 'lat', even)]
    pallas_call x9, Pallas kernels: 14.6 us -> 13.2 us  [call(): pl.pallas_call(kernel, out_shape=out_shape, in_specs=[pl.BlockSpec(memory...]
    ppermute x2, waiting for transfers between devices: 1.76 us -> 0.88 us  [lat_swap(): first = lax.ppermute(jnp.where(flag, up, dn), 'lat', even)]
  transfers between devices with their start and end apart: 10 -> 10, of which waited for: 6 -> 6; matrix products, arithmetic and copies ran while one was open for 0% -> 0% of each run, Pallas kernels for 7% -> 9%
where the time goes in v2:
time: 75.1 us; the launch traced here: 74.7 us
  blocking collectives  20.6 us (27%)
  starting transfers between devices  19.9 us (26%)
  Pallas kernels  18.2 us (24%)
  waiting for transfers between devices  12.3 us (16%)
  local copies, waits for them, and re-layouts  2.69 us (4%)
  between operations  0.81 us (1%)
    pallas_call x9, Pallas kernels, call(): pl.pallas_call(kernel, out_shape=out_shape, in_specs=[pl.BlockSpec(memory...  13.2 us
    all_to_all x1, blocking collectives, on_device(): stats = lax.all_to_all(stat, axes, 0, 0)  11.7 us
    all_to_all x1, blocking collectives, on_device(): sums = lax.all_to_all(sums, axes, 0, 0)  8.88 us
    ppermute x2, starting transfers between devices, lat_swap(): first = lax.ppermute(jnp.where(flag, up, dn), 'lat', even)  6.86 us
    pallas_call x2, Pallas kernels, backward(): pl.pallas_call(functools.partial(back_kernel, b), out_shape=S(state.shape...  4.96 us
    ppermute x2, starting transfers between devices, lon_swap(): second = lax.ppermute(side, 'lon', odd)  4.22 us
    all_to_all x1, starting transfers between devices, on_device(): parts = lax.all_to_all(wg, axes, 0, 0)  3.68 us
    all_to_all x1, waiting for transfers between devices, on_device(): parts = lax.all_to_all(wg, axes, 0, 0)  3.64 us
  transfers between devices with their start and end apart: 10, of which 6 were waited for; matrix products, arithmetic and copies ran while one was open for 0% of the time, Pallas kernels for 9%

profile of v2, /device:TPU:0, one launch (start us, length us, event | category | flops | bytes accessed | tf_op | source)
XLA Modules:
  0.0 74.7 jit_solution(695170910618613649)
XLA Ops:
  0.6 0.0 copy-start
  0.7 1.2 %copy-done = bf16[2,64,32,128]{3,2,1,0:T(8,128)(2,1)S(1)} copy-done((bf16[2,64,32,128]{3,2,1,0:T(8,128)(2,1)S(1)}, bf16[2,64,32,128]{3,2,1,0:T(8,128)(2,1)}, u32[]{:S(2)}) %copy-start) | copy-done | bytes 1048600
  1.9 0.0 copy-start.3
  1.9 0.7 copy-done.3
  2.6 0.0 copy-start.1
  2.6 0.0 copy-start.2
  2.6 0.1 shard_map.101
  2.7 0.8 %collective-permute-start.1 = (bf16[2,64,128]{2,1,0:T(8,128)(2,1)S(1)}, bf16[2,64,128]{2,1,0:T(8,128)(2,1)S(1)}, u32[]{:S(2)}, u32[]{:S(2)}) collective-permute-start(bf16[2,64,128]{2,1,0:T(8,128)(2,1)S(1)} %get-tuple-element.73), channel_id=1, source_target_pairs={{4,8},{8,4},{12,16},{16,12},{20,24},{24,20},{5,9},{9,5},{13,17},{1... | collective-permute-start | bytes 98312 | tf_op jit(solution)/shard_map/ppermute | solution.py:472
  3.5 4.4 %collective-permute-start = (bf16[2,64,128]{2,1,0:T(8,128)(2,1)S(1)}, bf16[2,64,128]{2,1,0:T(8,128)(2,1)S(1)}, u32[]{:S(2)}, u32[]{:S(2)}) collective-permute-start(bf16[2,64,128]{2,1,0:T(8,128)(2,1)S(1)} %get-tuple-element.74), channel_id=1, source_target_pairs={{0,4},{4,0},{8,12},{12,8},{16,20},{20,16},{24,28},{28,24},{1,5},{5... | collective-permute-start | bytes 98312 | tf_op jit(solution)/shard_map/ppermute | solution.py:473
  7.9 1.3 %shard_map.102 = (bf16[2,64,4096]{2,1,0:T(8,128)(2,1)S(1)}, bf16[64,128]{1,0:T(8,128)(2,1)S(1)}) custom-call(bf16[2,64,32,128]{3,2,1,0:T(8,128)(2,1)S(1)} %copy-done, f32[32,128]{1,0:T(8,128)S(1)} %get-tuple-element.35.maskf), custom_call_target="tpu_custom_call" | custom-call | bytes 2097152 | tf_op jit(solution)/shard_map/pallas_call | solution.py:34
  9.3 0.0 collective-permute-done.1
  9.3 0.0 collective-permute-done
  9.3 0.1 shard_map.103
  9.4 3.7 %collective-permute-start.3 = (bf16[2,64,128]{2,1,0:T(8,128)(2,1)S(1)}, bf16[2,64,128]{2,1,0:T(8,128)(2,1)S(1)}, u32[]{:S(2)}, u32[]{:S(2)}) collective-permute-start(bf16[2,64,128]{2,1,0:T(8,128)(2,1)S(1)} %shard_map.103), channel_id=1, source_target_pairs={{0,3},{1,2},{2,1},{3,0},{4,7},{5,6},{6,5},{7,4},{8,11},{9,10},{10,... | collective-permute-start | bytes 98312 | tf_op jit(solution)/shard_map/ppermute | solution.py:459
  13.0 0.0 collective-permute-start.2
  13.0 0.0 copy-done.1
  13.1 0.0 copy-done.2
  13.1 0.5 shard_map.104
  13.5 1.6 %collective-permute-done.3 = bf16[2,64,128]{2,1,0:T(8,128)(2,1)S(1)} collective-permute-done((bf16[2,64,128]{2,1,0:T(8,128)(2,1)S(1)}, bf16[2,64,128]{2,1,0:T(8,128)(2,1)S(1)}, u32[]{:S(2)}, u32[]{:S(2)}) %collective-permute-start.3) | collective-permute-done | bytes 32800 | tf_op jit(solution)/shard_map/ppermute | solution.py:459
  15.2 1.8 %collective-permute-done.2 = bf16[2,64,128]{2,1,0:T(8,128)(2,1)S(1)} collective-permute-done((bf16[2,64,128]{2,1,0:T(8,128)(2,1)S(1)}, bf16[2,64,128]{2,1,0:T(8,128)(2,1)S(1)}, u32[]{:S(2)}, u32[]{:S(2)}) %collective-permute-start.2) | collective-permute-done | bytes 32800 | tf_op jit(solution)/shard_map/ppermute | solution.py:458
  17.0 0.0 copy-start.4
  17.0 0.0 copy-start.5
  17.0 3.6 %shard_map.105 = (f32[2,64,4096]{2,1,0:T(8,128)S(1)}, bf16[2,64,4352]{2,1,0:T(8,128)(2,1)S(1)}, bf16[192,128]{1,0:T(8,128)(2,1)S(1)}, f32[32,2,128]{2,1,0:T(2,128)S(1)}) custom-call(bf16[2,64,4096]{2,1,0:T(8,128)(2,1)S(1)} %get-tuple-element.36.x_ref, bf16[2,64,128]{2,1,0:T(8,128)(2,1)S(1)} %get-tuple-element.72.above_ref, ...), custom_call_target="tpu_custom_call" | custom-call | flops 2415919104 | bytes 4194304 | tf_op jit(solution)/shard_map/pallas_call | solution.py:34
  20.6 11.7 %all_to_all.20.stat_ref = f32[32,2,128]{2,1,0:T(2,128)S(1)} all-to-all(f32[32,2,128]{2,1,0:T(2,128)S(1)} %get-tuple-element.41), channel_id=1, replica_groups=mesh['lat'=8,'lon'=4] {'lat','lon'}, dimensions={0} | all-to-all | bytes 65536 | tf_op jit(solution)/shard_map/all_to_all | solution.py:530
  32.3 0.0 copy-done.4
  32.3 0.0 copy-done.5
  32.3 2.9 %shard_map.106 = (bf16[2,64,32,128]{3,2,1,0:T(8,128)(2,1)}, f32[2,64,4096]{2,1,0:T(8,128)S(1)}, f32[64,128]{1,0:T(8,128)S(1)}, f32[32,1,128]{2,1,0:T(1,128)S(1)}) custom-call(f32[32,2,128]{2,1,0:T(2,128)S(1)} %all_to_all.20.stat_ref, f32[2,64,4096]{2,1,0:T(8,128)S(1)} %get-tuple-element.42.conv_ref, bf16[2,64,4096]{2,1,0:T(8,128)(2,1)S(1)} %get-tuple-element.43.cot_ref, ...), custom_call_target="tpu_custom_call" | custom-call | flops 20971520 | bytes 6291456 | tf_op jit(solution)/shard_map/pallas_call | solution.py:34
  35.2 8.9 %all_to_all.21.sum_ref = f32[32,1,128]{2,1,0:T(1,128)S(1)} all-to-all(f32[32,1,128]{2,1,0:T(1,128)S(1)} %get-tuple-element.45), channel_id=1, replica_groups=mesh['lat'=8,'lon'=4] {'lat','lon'}, dimensions={0} | all-to-all | bytes 32768 | tf_op jit(solution)/shard_map/all_to_all | solution.py:539
  44.1 3.8 %shard_map.107 = (bf16[2,64,4096]{2,1,0:T(8,128)(2,1)S(1)}, bf16[2,64,128]{2,1,0:T(8,128)(2,1)S(1)}, bf16[2,64,128]{2,1,0:T(8,128)(2,1)S(1)}, bf16[64,128]{1,0:T...) custom-call(f32[32,1,128]{2,1,0:T(1,128)S(1)} %all_to_all.21.sum_ref, ...), custom_call_target="tpu_custom_call" | custom-call | flops 2415919104 | bytes 6291456 | tf_op jit(solution)/shard_map/pallas_call | solution.py:34
  47.9 0.6 collective-permute-start.5
  48.4 0.5 collective-permute-start.4
  49.0 3.7 %all-to-all-start.2 = ((f32[32,1,1152]{2,1,0:T(1,128)}), f32[32,1,1152]{2,1,0:T(1,128)S(1)}, u32[]{:S(2)}, u32[]{:S(2)}) async-start(f32[32,1,1152]{2,1,0:T(1,128)} %get-tuple-element.51), calls=%async_computation.2 | async-start | bytes 294912 | tf_op jit(solution)/shard_map/all_to_all | solution.py:555
  52.7 0.8 %collective-permute-done.5 = bf16[64,128]{1,0:T(8,128)(2,1)S(1)} collective-permute-done((bf16[64,128]{1,0:T(8,128)(2,1)S(1)}, bf16[64,128]{1,0:T(8,128)(2,1)S(1)}, u32[]{:S(2)}, u32[]{:S(2)}) %collective-permute-start.5) | collective-permute-done | bytes 16416 | tf_op jit(solution)/shard_map/ppermute | solution.py:459
  53.4 0.0 collective-permute-done.4
  53.4 0.2 shard_map.108
  53.6 0.7 collective-permute-start.7
  54.3 2.5 %collective-permute-start.6 = (bf16[3,64,128]{2,1,0:T(8,128)(2,1)S(1)}, bf16[3,64,128]{2,1,0:T(8,128)(2,1)S(1)}, u32[]{:S(2)}, u32[]{:S(2)}) collective-permute-start(bf16[3,64,128]{2,1,0:T(8,128)(2,1)S(1)} %get-tuple-element.68), channel_id=1, source_target_pairs={{0,4},{4,0},{8,12},{12,8},{16,20},{20,16},{24,28},{28,24},{1,5},{5... | collective-permute-start | bytes 147464 | tf_op jit(solution)/shard_map/ppermute | solution.py:473
  56.7 0.0 collective-permute-done.7
  56.7 0.9 %collective-permute-done.6 = bf16[3,64,128]{2,1,0:T(8,128)(2,1)S(1)} collective-permute-done((bf16[3,64,128]{2,1,0:T(8,128)(2,1)S(1)}, bf16[3,64,128]{2,1,0:T(8,128)(2,1)S(1)}, u32[]{:S(2)}, u32[]{:S(2)}) %collective-permute-start.6) | collective-permute-done | bytes 49184 | tf_op jit(solution)/shard_map/ppermute | solution.py:473
  57.6 3.6 %all-to-all-done.2 = f32[32,1,1152]{2,1,0:T(1,128)S(1)} async-done(((f32[32,1,1152]{2,1,0:T(1,128)}), f32[32,1,1152]{2,1,0:T(1,128)S(1)}, u32[]{:S(2)}, u32[]{:S(2)}) %all-to-all-start.2) | async-done | bytes 147488 | tf_op jit(solution)/shard_map/all_to_all | solution.py:555
  61.3 0.1 reduce_sum.9
  61.4 0.7 broadcast_in_dim.14
  62.1 3.1 %all-to-all-start.3 = ((f32[32,1,1152]{2,1,0:T(1,128)}), f32[32,1,1152]{2,1,0:T(1,128)S(1)}, u32[]{:S(2)}, u32[]{:S(2)}) async-start(f32[32,1,1152]{2,1,0:T(1,128)} %broadcast_in_dim.14), calls=%async_computation.3 | async-start | bytes 294912 | tf_op jit(solution)/shard_map/all_to_all | solution.py:560
  65.3 2.5 %shard_map.109.rest_0_ = bf16[2,64,32,128]{3,2,1,0:T(8,128)(2,1)} custom-call(bf16[2,64,4096]{2,1,0:T(8,128)(2,1)S(1)} %get-tuple-element.50.d_ref, bf16[3,64,128]{2,1,0:T(8,128)(2,1)S(1)} %get-tuple-element.58.above_ref, bf16[3,64,128]{2,1,0:T(8,128)(2,1)S(1)} %get-tuple-element.59.below_ref, bf16[64,128]{1,0:T(8,128)(2,1)S(1)} %get-tuple-element.60.edge_ref, ...), custom_call_target="tpu_custom_call" | custom-call | flops 1207959552 | bytes 2097152 | tf_op jit(solution)/shard_map/pallas_call | solution.py:567
  67.8 2.5 %shard_map.110 = bf16[2,64,32,128]{3,2,1,0:T(8,128)(2,1)} custom-call(bf16[2,64,4096]{2,1,0:T(8,128)(2,1)S(1)} %get-tuple-element.50.d_ref, bf16[3,64,128]{2,1,0:T(8,128)(2,1)S(1)} %get-tuple-element.58.above_ref, bf16[3,64,128]{2,1,0:T(8,128)(2,1)S(1)} %get-tuple-element.59.below_ref, ...), custom_call_target="tpu_custom_call", output_to_operand_aliasing={{}: (6, {})} | custom-call | flops 1207959552 | bytes 2097152 | tf_op jit(solution)/shard_map/pallas_call | solution.py:567
  70.2 3.6 %all-to-all-done.3.x_ref = f32[32,1,1152]{2,1,0:T(1,128)S(1)} async-done(((f32[32,1,1152]{2,1,0:T(1,128)}), f32[32,1,1152]{2,1,0:T(1,128)S(1)}, u32[]{:S(2)}, u32[]{:S(2)}) %all-to-all-start.3) | async-done | bytes 147488 | tf_op jit(solution)/shard_map/all_to_all | solution.py:560
  73.9 0.8 %shard_map.111 = f32[3,3,64,64]{3,2,1,0:T(8,128)} custom-call(f32[32,1,1152]{2,1,0:T(1,128)S(1)} %all-to-all-done.3.x_ref), custom_call_target="tpu_custom_call" | custom-call | bytes 500000 | tf_op jit(solution)/shard_map/pallas_call | solution.py:34
  (6 shorter events, 0.1 us)
Async XLA Ops:
  0.6 1.2 %copy-start = (bf16[2,64,32,128]{3,2,1,0:T(8,128)(2,1)S(1)}, bf16[2,64,32,128]{3,2,1,0:T(8,128)(2,1)}, u32[]{:S(2)}) copy-start(bf16[2,64,32,128]{3,2,1,0:T(8,128)(2,1)} %x_ref.4) | copy-start | bytes 3145732
  1.9 0.7 copy-start.3
  2.6 10.5 %copy-start.1 = (bf16[2,64,32,128]{3,2,1,0:T(8,128)(2,1)S(1)}, bf16[2,64,32,128]{3,2,1,0:T(8,128)(2,1)}, u32[]{:S(2)}) copy-start(bf16[2,64,32,128]{3,2,1,0:T(8,128)(2,1)} %x_ref.5) | copy-start | bytes 3145732
  2.6 10.5 %copy-start.2 = (bf16[3,3,64,64]{3,2,1,0:T(8,128)(2,1)S(1)}, bf16[3,3,64,64]{3,2,1,0:T(8,128)(2,1)}, u32[]{:S(2)}) copy-start(bf16[3,3,64,64]{3,2,1,0:T(8,128)(2,1)} %w_ref.1) | copy-start | bytes 221188
  2.7 6.6 %collective-permute-start.1 = (bf16[2,64,128]{2,1,0:T(8,128)(2,1)S(1)}, bf16[2,64,128]{2,1,0:T(8,128)(2,1)S(1)}, u32[]{:S(2)}, u32[]{:S(2)}) collective-permute-start(bf16[2,64,128]{2,1,0:T(8,128)(2,1)S(1)} %get-tuple-element.73), channel_id=1, source_target_pairs={{4,8},{8,4},{12,16},{16,12},{20,24},{24,20},{5,9},{9,5},{13,17},{1... | collective-permute-start | bytes 98312 | tf_op jit(solution)/shard_map/ppermute | solution.py:472
  3.5 5.8 %collective-permute-start = (bf16[2,64,128]{2,1,0:T(8,128)(2,1)S(1)}, bf16[2,64,128]{2,1,0:T(8,128)(2,1)S(1)}, u32[]{:S(2)}, u32[]{:S(2)}) collective-permute-start(bf16[2,64,128]{2,1,0:T(8,128)(2,1)S(1)} %get-tuple-element.74), channel_id=1, source_target_pairs={{0,4},{4,0},{8,12},{12,8},{16,20},{20,16},{24,28},{28,24},{1,5},{5... | collective-permute-start | bytes 98312 | tf_op jit(solution)/shard_map/ppermute | solution.py:473
  9.4 5.8 %collective-permute-start.3 = (bf16[2,64,128]{2,1,0:T(8,128)(2,1)S(1)}, bf16[2,64,128]{2,1,0:T(8,128)(2,1)S(1)}, u32[]{:S(2)}, u32[]{:S(2)}) collective-permute-start(bf16[2,64,128]{2,1,0:T(8,128)(2,1)S(1)} %shard_map.103), channel_id=1, source_target_pairs={{0,3},{1,2},{2,1},{3,0},{4,7},{5,6},{6,5},{7,4},{8,11},{9,10},{10,... | collective-permute-start | bytes 98312 | tf_op jit(solution)/shard_map/ppermute | solution.py:459
  13.0 3.9 %collective-permute-start.2 = (bf16[2,64,128]{2,1,0:T(8,128)(2,1)S(1)}, bf16[2,64,128]{2,1,0:T(8,128)(2,1)S(1)}, u32[]{:S(2)}, u32[]{:S(2)}) collective-permute-start(bf16[2,64,128]{2,1,0:T(8,128)(2,1)S(1)} %shard_map.103), channel_id=1, source_target_pairs={{0,1},{1,0},{2,3},{3,2},{4,5},{5,4},{6,7},{7,6},{8,9},{9,8},{10,11... | collective-permute-start | bytes 98312 | tf_op jit(solution)/shard_map/ppermute | solution.py:458
  17.0 15.3 %copy-start.4 = (f32[64]{0:T(128)S(1)}, f32[64]{0:T(128)}, u32[]{:S(2)}) copy-start(f32[64]{0:T(128)} %param.9) | copy-start | bytes 772
  17.0 15.3 %copy-start.5 = (f32[64]{0:T(128)S(1)}, f32[64]{0:T(128)}, u32[]{:S(2)}) copy-start(f32[64]{0:T(128)} %param.10) | copy-start | bytes 772
  47.9 5.5 %collective-permute-start.5 = (bf16[64,128]{1,0:T(8,128)(2,1)S(1)}, bf16[64,128]{1,0:T(8,128)(2,1)S(1)}, u32[]{:S(2)}, u32[]{:S(2)}) collective-permute-start(bf16[64,128]{1,0:T(8,128)(2,1)S(1)} %get-tuple-element.54), channel_id=1, source_target_pairs={{0,3},{1,2},{2,1},{3,0},{4,7},{5,6},{6,5},{7,4},{8,11},{9,10},{10,... | collective-permute-start | bytes 49160 | tf_op jit(solution)/shard_map/ppermute | solution.py:459
  48.4 5.0 %collective-permute-start.4 = (bf16[64,128]{1,0:T(8,128)(2,1)S(1)}, bf16[64,128]{1,0:T(8,128)(2,1)S(1)}, u32[]{:S(2)}, u32[]{:S(2)}) collective-permute-start(bf16[64,128]{1,0:T(8,128)(2,1)S(1)} %get-tuple-element.54), channel_id=1, source_target_pairs={{0,1},{1,0},{2,3},{3,2},{4,5},{5,4},{6,7},{7,6},{8,9},{9,8},{10,11... | collective-permute-start | bytes 49160 | tf_op jit(solution)/shard_map/ppermute | solution.py:458
  49.0 12.3 %all-to-all-start.2 = ((f32[32,1,1152]{2,1,0:T(1,128)}), f32[32,1,1152]{2,1,0:T(1,128)S(1)}, u32[]{:S(2)}, u32[]{:S(2)}) async-start(f32[32,1,1152]{2,1,0:T(1,128)} %get-tuple-element.51), calls=%async_computation.2 | async-start | bytes 294912 | tf_op jit(solution)/shard_map/all_to_all | solution.py:555
  53.6 3.1 %collective-permute-start.7 = (bf16[3,64,128]{2,1,0:T(8,128)(2,1)S(1)}, bf16[3,64,128]{2,1,0:T(8,128)(2,1)S(1)}, u32[]{:S(2)}, u32[]{:S(2)}) collective-permute-start(bf16[3,64,128]{2,1,0:T(8,128)(2,1)S(1)} %get-tuple-element.67), channel_id=1, source_target_pairs={{4,8},{8,4},{12,16},{16,12},{20,24},{24,20},{5,9},{9,5},{13,17},{1... | collective-permute-start | bytes 147464 | tf_op jit(solution)/shard_map/ppermute | solution.py:472
  54.3 3.3 %collective-permute-start.6 = (bf16[3,64,128]{2,1,0:T(8,128)(2,1)S(1)}, bf16[3,64,128]{2,1,0:T(8,128)(2,1)S(1)}, u32[]{:S(2)}, u32[]{:S(2)}) collective-permute-start(bf16[3,64,128]{2,1,0:T(8,128)(2,1)S(1)} %get-tuple-element.68), channel_id=1, source_target_pairs={{0,4},{4,0},{8,12},{12,8},{16,20},{20,16},{24,28},{28,24},{1,5},{5... | collective-permute-start | bytes 147464 | tf_op jit(solution)/shard_map/ppermute | solution.py:473
  62.1 11.7 %all-to-all-start.3 = ((f32[32,1,1152]{2,1,0:T(1,128)}), f32[32,1,1152]{2,1,0:T(1,128)S(1)}, u32[]{:S(2)}, u32[]{:S(2)}) async-start(f32[32,1,1152]{2,1,0:T(1,128)} %broadcast_in_dim.14), calls=%async_computation.3 | async-start | bytes 294912 | tf_op jit(solution)/shard_map/all_to_all | solution.py:560

commit v3 on v2

--- a/solution.py
+++ b/solution.py
@@ -274,7 +274,7 @@
 
 
 def silu_kernel(
-    stat_ref, conv_ref, cot_ref, maskf, gain_ref, bias_ref, act_ref, dpre_ref, par_ref, sum_ref, tmp
+    stat_ref, conv_ref, cot_ref, maskf, gain_ref, bias_ref, act_ref, dpre_ref, par_ref, sum_ref
 ):
     batch, chans, _ = conv_ref.shape
     high, width = maskf.shape
@@ -302,7 +302,7 @@
             t = jnp.tanh(half)
             s = 0.5 + 0.5 * t
             act = half + half * t
-            tmp[channel_rows(b, h, chans, high), :] = act * maskf[pl.ds(h, 1), :]
+            act_ref[b, :, at] = (act * maskf[pl.ds(h, 1), :]).astype(BF16)
             dpre = cot_ref[b, :, at].astype(F32) * (s + act * (0.5 - 0.5 * t))
             dpre_ref[b, :, at] = dpre
             return sums[0] + dpre, sums[1] + dpre * dev
@@ -310,8 +310,18 @@
         sums = lax.fori_loop(0, high, row, sums, unroll=4)
     total = lanes_sum(sums[0], sums[1] * column(cols, 1, width))
     sum_ref[...] = jnp.broadcast_to(total[None], sum_ref.shape)
-    for b in range(batch):
-        pack_rows(tmp.at[b * chans * (high + 1) : (b + 1) * chans * (high + 1)], act_ref.at[b], chans, high)
+
+
+def pack_kernel(act_ref, out_ref, tmp):
+    batch, chans, high, width = out_ref.shape
+    for b in range(batch):
+
+        def row(h, carry, b=b):
+            tmp[channel_rows(b, h, chans, high), :] = act_ref[b, :, row_lanes(h, width)].astype(F32)
+            return carry
+
+        lax.fori_loop(0, high, row, 0, unroll=8)
+        pack_rows(tmp.at[b * chans * (high + 1) : (b + 1) * chans * (high + 1)], out_ref.at[b], chans, high)
 
 
 def grad_kernel(
@@ -528,15 +538,16 @@
         xm, above, below, left, right, w_fwd, flag,
     )
     stats = lax.all_to_all(stat, axes, 0, 0)
-    activated, dpre, par, sums = call(
+    active, dpre, par, sums = call(
         silu_kernel,
-        (S(state.shape, BF16), wide, S((chans, width), F32), S((devices, 1, 2 * chans), F32)),
-        [tmp],
+        (plane, wide, S((chans, width), F32), S((devices, 1, 2 * chans), F32)),
+        [],
         20 * size,
         6 * size,
         stats, conv, cot, flag, norm_gain[None], batchnorm_bias[None],
     )
     sums = lax.all_to_all(sums, axes, 0, 0)
+    activated = call(pack_kernel, S(state.shape, BF16), [tmp], 0, 3 * size, active)
     stacked = pltpu.VMEM((3 * chans, GROUP * width), BF16)
     share = -(-9 * chans * chans // (width * devices))
     flatg = pltpu.VMEM((share * devices, width), F32)

time: 75.1 us -> 74.2 us (0.988)
  waiting for transfers between devices: 12.3 us -> 11 us
    all_to_all x1, waiting for transfers between devices: 3.63 us -> 2.28 us  [on_device(): wg = lax.all_to_all(shares, axes, 0, 0)]
    pallas_call x9 -> x10, Pallas kernels: 13.2 us -> 13.7 us  [call(): pl.pallas_call(kernel, out_shape=out_shape, in_specs=[pl.BlockSpec(memory...]
  transfers between devices with their start and end apart: 10 -> 10, of which waited for: 6 -> 6; matrix products, arithmetic and copies ran while one was open for 0% -> 0% of each run, Pallas kernels for 9% -> 11%
where the time goes in v3:
time: 74.2 us; the launch traced here: 73.9 us
  blocking collectives  20.6 us (28%)
  starting transfers between devices  19.9 us (27%)
  Pallas kernels  18.7 us (25%)
  waiting for transfers between devices  11 us (15%)
  local copies, waits for them, and re-layouts  2.69 us (4%)
  between operations  0.82 us (1%)
    pallas_call x10, Pallas kernels, call(): pl.pallas_call(kernel, out_shape=out_shape, in_specs=[pl.BlockSpec(memory...  13.7 us
    all_to_all x1, blocking collectives, on_device(): stats = lax.all_to_all(stat, axes, 0, 0)  11.7 us
    all_to_all x1, blocking collectives, on_device(): sums = lax.all_to_all(sums, axes, 0, 0)  8.89 us
    ppermute x2, starting transfers between devices, lat_swap(): first = lax.ppermute(jnp.where(flag, up, dn), 'lat', even)  6.86 us
    pallas_call x2, Pallas kernels, backward(): pl.pallas_call(functools.partial(back_kernel, b), out_shape=S(state.shape...  4.93 us
    ppermute x2, starting transfers between devices, lon_swap(): second = lax.ppermute(side, 'lon', odd)  4.22 us
    all_to_all x1, starting transfers between devices, on_device(): parts = lax.all_to_all(wg, axes, 0, 0)  3.68 us
    all_to_all x1, waiting for transfers between devices, on_device(): parts = lax.all_to_all(wg, axes, 0, 0)  3.64 us
  transfers between devices with their start and end apart: 10, of which 6 were waited for; matrix products, arithmetic and copies ran while one was open for 0% of the time, Pallas kernels for 11%

profile of v3, /device:TPU:0, one launch (start us, length us, event | category | flops | bytes accessed | tf_op | source)
XLA Modules:
  0.0 73.9 jit_solution(3778414875841502310)
XLA Ops:
  0.6 0.0 copy-start
  0.7 1.2 %copy-done = bf16[2,64,32,128]{3,2,1,0:T(8,128)(2,1)S(1)} copy-done((bf16[2,64,32,128]{3,2,1,0:T(8,128)(2,1)S(1)}, bf16[2,64,32,128]{3,2,1,0:T(8,128)(2,1)}, u32[]{:S(2)}) %copy-start) | copy-done | bytes 1048600
  1.9 0.0 copy-start.3
  1.9 0.7 copy-done.3
  2.6 0.0 copy-start.1
  2.6 0.0 copy-start.2
  2.6 0.1 shard_map.101
  2.7 0.8 %collective-permute-start.1 = (bf16[2,64,128]{2,1,0:T(8,128)(2,1)S(1)}, bf16[2,64,128]{2,1,0:T(8,128)(2,1)S(1)}, u32[]{:S(2)}, u32[]{:S(2)}) collective-permute-start(bf16[2,64,128]{2,1,0:T(8,128)(2,1)S(1)} %get-tuple-element.73), channel_id=1, source_target_pairs={{4,8},{8,4},{12,16},{16,12},{20,24},{24,20},{5,9},{9,5},{13,17},{1... | collective-permute-start | bytes 98312 | tf_op jit(solution)/shard_map/ppermute | solution.py:482
  3.5 4.4 %collective-permute-start = (bf16[2,64,128]{2,1,0:T(8,128)(2,1)S(1)}, bf16[2,64,128]{2,1,0:T(8,128)(2,1)S(1)}, u32[]{:S(2)}, u32[]{:S(2)}) collective-permute-start(bf16[2,64,128]{2,1,0:T(8,128)(2,1)S(1)} %get-tuple-element.74), channel_id=1, source_target_pairs={{0,4},{4,0},{8,12},{12,8},{16,20},{20,16},{24,28},{28,24},{1,5},{5... | collective-permute-start | bytes 98312 | tf_op jit(solution)/shard_map/ppermute | solution.py:483
  7.9 1.3 %shard_map.102 = (bf16[2,64,4096]{2,1,0:T(8,128)(2,1)S(1)}, bf16[64,128]{1,0:T(8,128)(2,1)S(1)}) custom-call(bf16[2,64,32,128]{3,2,1,0:T(8,128)(2,1)S(1)} %copy-done, f32[32,128]{1,0:T(8,128)S(1)} %get-tuple-element.35.maskf), custom_call_target="tpu_custom_call" | custom-call | bytes 2097152 | tf_op jit(solution)/shard_map/pallas_call | solution.py:34
  9.3 0.0 collective-permute-done.1
  9.3 0.0 collective-permute-done
  9.3 0.1 shard_map.103
  9.4 3.7 %collective-permute-start.3 = (bf16[2,64,128]{2,1,0:T(8,128)(2,1)S(1)}, bf16[2,64,128]{2,1,0:T(8,128)(2,1)S(1)}, u32[]{:S(2)}, u32[]{:S(2)}) collective-permute-start(bf16[2,64,128]{2,1,0:T(8,128)(2,1)S(1)} %shard_map.103), channel_id=1, source_target_pairs={{0,3},{1,2},{2,1},{3,0},{4,7},{5,6},{6,5},{7,4},{8,11},{9,10},{10,... | collective-permute-start | bytes 98312 | tf_op jit(solution)/shard_map/ppermute | solution.py:469
  13.0 0.0 collective-permute-start.2
  13.0 0.0 copy-done.1
  13.1 0.0 copy-done.2
  13.1 0.5 shard_map.104
  13.5 1.6 %collective-permute-done.3 = bf16[2,64,128]{2,1,0:T(8,128)(2,1)S(1)} collective-permute-done((bf16[2,64,128]{2,1,0:T(8,128)(2,1)S(1)}, bf16[2,64,128]{2,1,0:T(8,128)(2,1)S(1)}, u32[]{:S(2)}, u32[]{:S(2)}) %collective-permute-start.3) | collective-permute-done | bytes 32800 | tf_op jit(solution)/shard_map/ppermute | solution.py:469
  15.2 1.8 %collective-permute-done.2 = bf16[2,64,128]{2,1,0:T(8,128)(2,1)S(1)} collective-permute-done((bf16[2,64,128]{2,1,0:T(8,128)(2,1)S(1)}, bf16[2,64,128]{2,1,0:T(8,128)(2,1)S(1)}, u32[]{:S(2)}, u32[]{:S(2)}) %collective-permute-start.2) | collective-permute-done | bytes 32800 | tf_op jit(solution)/shard_map/ppermute | solution.py:468
  17.0 0.0 copy-start.4
  17.0 0.0 copy-start.5
  17.0 3.5 %shard_map.105 = (f32[2,64,4096]{2,1,0:T(8,128)S(1)}, bf16[2,64,4352]{2,1,0:T(8,128)(2,1)S(1)}, bf16[192,128]{1,0:T(8,128)(2,1)S(1)}, f32[32,2,128]{2,1,0:T(2,128)S(1)}) custom-call(bf16[2,64,4096]{2,1,0:T(8,128)(2,1)S(1)} %get-tuple-element.36.x_ref, bf16[2,64,128]{2,1,0:T(8,128)(2,1)S(1)} %get-tuple-element.72.above_ref, ...), custom_call_target="tpu_custom_call" | custom-call | flops 2415919104 | bytes 4194304 | tf_op jit(solution)/shard_map/pallas_call | solution.py:34
  20.5 11.7 %all_to_all.20.stat_ref = f32[32,2,128]{2,1,0:T(2,128)S(1)} all-to-all(f32[32,2,128]{2,1,0:T(2,128)S(1)} %get-tuple-element.41), channel_id=1, replica_groups=mesh['lat'=8,'lon'=4] {'lat','lon'}, dimensions={0} | all-to-all | bytes 65536 | tf_op jit(solution)/shard_map/all_to_all | solution.py:540
  32.3 0.0 copy-done.4
  32.3 0.0 copy-done.5
  32.3 2.1 %shard_map.106 = (bf16[2,64,4096]{2,1,0:T(8,128)(2,1)S(1)}, f32[2,64,4096]{2,1,0:T(8,128)S(1)}, f32[64,128]{1,0:T(8,128)S(1)}, f32[32,1,128]{2,1,0:T(1,128)S(1)}) custom-call(f32[32,2,128]{2,1,0:T(2,128)S(1)} %all_to_all.20.stat_ref, f32[2,64,4096]{2,1,0:T(8,128)S(1)} %get-tuple-element.42.conv_ref, bf16[2,64,4096]{2,1,0:T(8,128)(2,1)S(1)} %get-tuple-element.43.cot_ref, ...), custom_call_target="tpu_custom_call" | custom-call | flops 20971520 | bytes 6291456 | tf_op jit(solution)/shard_map/pallas_call | solution.py:34
  34.4 8.9 %all_to_all.21.sum_ref = f32[32,1,128]{2,1,0:T(1,128)S(1)} all-to-all(f32[32,1,128]{2,1,0:T(1,128)S(1)} %get-tuple-element.45), channel_id=1, replica_groups=mesh['lat'=8,'lon'=4] {'lat','lon'}, dimensions={0} | all-to-all | bytes 32768 | tf_op jit(solution)/shard_map/all_to_all | solution.py:549
  43.3 3.8 %shard_map.108 = (bf16[2,64,4096]{2,1,0:T(8,128)(2,1)S(1)}, bf16[2,64,128]{2,1,0:T(8,128)(2,1)S(1)}, bf16[2,64,128]{2,1,0:T(8,128)(2,1)S(1)}, bf16[64,128]{1,0:T...) custom-call(f32[32,1,128]{2,1,0:T(1,128)S(1)} %all_to_all.21.sum_ref, ...), custom_call_target="tpu_custom_call" | custom-call | flops 2415919104 | bytes 6291456 | tf_op jit(solution)/shard_map/pallas_call | solution.py:34
  47.0 0.6 collective-permute-start.5
  47.6 0.5 collective-permute-start.4
  48.1 3.7 %all-to-all-start.2 = ((f32[32,1,1152]{2,1,0:T(1,128)}), f32[32,1,1152]{2,1,0:T(1,128)S(1)}, u32[]{:S(2)}, u32[]{:S(2)}) async-start(f32[32,1,1152]{2,1,0:T(1,128)} %get-tuple-element.51), calls=%async_computation.2 | async-start | bytes 294912 | tf_op jit(solution)/shard_map/all_to_all | solution.py:566
  51.8 0.7 %collective-permute-done.5 = bf16[64,128]{1,0:T(8,128)(2,1)S(1)} collective-permute-done((bf16[64,128]{1,0:T(8,128)(2,1)S(1)}, bf16[64,128]{1,0:T(8,128)(2,1)S(1)}, u32[]{:S(2)}, u32[]{:S(2)}) %collective-permute-start.5) | collective-permute-done | bytes 16416 | tf_op jit(solution)/shard_map/ppermute | solution.py:469
  52.6 0.0 collective-permute-done.4
  52.6 0.2 shard_map.109
  52.8 0.7 collective-permute-start.7
  53.4 2.5 %collective-permute-start.6 = (bf16[3,64,128]{2,1,0:T(8,128)(2,1)S(1)}, bf16[3,64,128]{2,1,0:T(8,128)(2,1)S(1)}, u32[]{:S(2)}, u32[]{:S(2)}) collective-permute-start(bf16[3,64,128]{2,1,0:T(8,128)(2,1)S(1)} %get-tuple-element.68), channel_id=1, source_target_pairs={{0,4},{4,0},{8,12},{12,8},{16,20},{20,16},{24,28},{28,24},{1,5},{5... | collective-permute-start | bytes 147464 | tf_op jit(solution)/shard_map/ppermute | solution.py:483
  55.9 0.0 collective-permute-done.7
  55.9 0.9 %collective-permute-done.6 = bf16[3,64,128]{2,1,0:T(8,128)(2,1)S(1)} collective-permute-done((bf16[3,64,128]{2,1,0:T(8,128)(2,1)S(1)}, bf16[3,64,128]{2,1,0:T(8,128)(2,1)S(1)}, u32[]{:S(2)}, u32[]{:S(2)}) %collective-permute-start.6) | collective-permute-done | bytes 49184 | tf_op jit(solution)/shard_map/ppermute | solution.py:483
  56.8 3.6 %all-to-all-done.2 = f32[32,1,1152]{2,1,0:T(1,128)S(1)} async-done(((f32[32,1,1152]{2,1,0:T(1,128)}), f32[32,1,1152]{2,1,0:T(1,128)S(1)}, u32[]{:S(2)}, u32[]{:S(2)}) %all-to-all-start.2) | async-done | bytes 147488 | tf_op jit(solution)/shard_map/all_to_all | solution.py:566
  60.4 0.1 reduce_sum.9
  60.5 0.7 broadcast_in_dim.14
  61.3 3.1 %all-to-all-start.3 = ((f32[32,1,1152]{2,1,0:T(1,128)}), f32[32,1,1152]{2,1,0:T(1,128)S(1)}, u32[]{:S(2)}, u32[]{:S(2)}) async-start(f32[32,1,1152]{2,1,0:T(1,128)} %broadcast_in_dim.14), calls=%async_computation.3 | async-start | bytes 294912 | tf_op jit(solution)/shard_map/all_to_all | solution.py:571
  64.4 1.4 %shard_map.107 = bf16[2,64,32,128]{3,2,1,0:T(8,128)(2,1)} custom-call(bf16[2,64,4096]{2,1,0:T(8,128)(2,1)S(1)} %get-tuple-element.44.act_ref), custom_call_target="tpu_custom_call" | custom-call | bytes 3145728 | tf_op jit(solution)/shard_map/pallas_call | solution.py:34
  65.8 2.5 %shard_map.110.rest_0_ = bf16[2,64,32,128]{3,2,1,0:T(8,128)(2,1)} custom-call(bf16[2,64,4096]{2,1,0:T(8,128)(2,1)S(1)} %get-tuple-element.50.d_ref, bf16[3,64,128]{2,1,0:T(8,128)(2,1)S(1)} %get-tuple-element.58.above_ref, bf16[3,64,128]{2,1,0:T(8,128)(2,1)S(1)} %get-tuple-element.59.below_ref, bf16[64,128]{1,0:T(8,128)(2,1)S(1)} %get-tuple-element.60.edge_ref, ...), custom_call_target="tpu_custom_call" | custom-call | flops 1207959552 | bytes 2097152 | tf_op jit(solution)/shard_map/pallas_call | solution.py:578
  68.3 2.5 %shard_map.111 = bf16[2,64,32,128]{3,2,1,0:T(8,128)(2,1)} custom-call(bf16[2,64,4096]{2,1,0:T(8,128)(2,1)S(1)} %get-tuple-element.50.d_ref, bf16[3,64,128]{2,1,0:T(8,128)(2,1)S(1)} %get-tuple-element.58.above_ref, bf16[3,64,128]{2,1,0:T(8,128)(2,1)S(1)} %get-tuple-element.59.below_ref, ...), custom_call_target="tpu_custom_call", output_to_operand_aliasing={{}: (6, {})} | custom-call | flops 1207959552 | bytes 2097152 | tf_op jit(solution)/shard_map/pallas_call | solution.py:578
  70.7 2.3 %all-to-all-done.3.x_ref = f32[32,1,1152]{2,1,0:T(1,128)S(1)} async-done(((f32[32,1,1152]{2,1,0:T(1,128)}), f32[32,1,1152]{2,1,0:T(1,128)S(1)}, u32[]{:S(2)}, u32[]{:S(2)}) %all-to-all-start.3) | async-done | bytes 147488 | tf_op jit(solution)/shard_map/all_to_all | solution.py:571
  73.0 0.8 %shard_map.112 = f32[3,3,64,64]{3,2,1,0:T(8,128)} custom-call(f32[32,1,1152]{2,1,0:T(1,128)S(1)} %all-to-all-done.3.x_ref), custom_call_target="tpu_custom_call" | custom-call | bytes 500000 | tf_op jit(solution)/shard_map/pallas_call | solution.py:34
  (6 shorter events, 0.1 us)
Async XLA Ops:
  0.6 1.2 %copy-start = (bf16[2,64,32,128]{3,2,1,0:T(8,128)(2,1)S(1)}, bf16[2,64,32,128]{3,2,1,0:T(8,128)(2,1)}, u32[]{:S(2)}) copy-start(bf16[2,64,32,128]{3,2,1,0:T(8,128)(2,1)} %x_ref.4) | copy-start | bytes 3145732
  1.9 0.7 copy-start.3
  2.6 10.5 %copy-start.1 = (bf16[2,64,32,128]{3,2,1,0:T(8,128)(2,1)S(1)}, bf16[2,64,32,128]{3,2,1,0:T(8,128)(2,1)}, u32[]{:S(2)}) copy-start(bf16[2,64,32,128]{3,2,1,0:T(8,128)(2,1)} %x_ref.5) | copy-start | bytes 3145732
  2.6 10.5 %copy-start.2 = (bf16[3,3,64,64]{3,2,1,0:T(8,128)(2,1)S(1)}, bf16[3,3,64,64]{3,2,1,0:T(8,128)(2,1)}, u32[]{:S(2)}) copy-start(bf16[3,3,64,64]{3,2,1,0:T(8,128)(2,1)} %w_ref.1) | copy-start | bytes 221188
  2.7 6.6 %collective-permute-start.1 = (bf16[2,64,128]{2,1,0:T(8,128)(2,1)S(1)}, bf16[2,64,128]{2,1,0:T(8,128)(2,1)S(1)}, u32[]{:S(2)}, u32[]{:S(2)}) collective-permute-start(bf16[2,64,128]{2,1,0:T(8,128)(2,1)S(1)} %get-tuple-element.73), channel_id=1, source_target_pairs={{4,8},{8,4},{12,16},{16,12},{20,24},{24,20},{5,9},{9,5},{13,17},{1... | collective-permute-start | bytes 98312 | tf_op jit(solution)/shard_map/ppermute | solution.py:482
  3.5 5.8 %collective-permute-start = (bf16[2,64,128]{2,1,0:T(8,128)(2,1)S(1)}, bf16[2,64,128]{2,1,0:T(8,128)(2,1)S(1)}, u32[]{:S(2)}, u32[]{:S(2)}) collective-permute-start(bf16[2,64,128]{2,1,0:T(8,128)(2,1)S(1)} %get-tuple-element.74), channel_id=1, source_target_pairs={{0,4},{4,0},{8,12},{12,8},{16,20},{20,16},{24,28},{28,24},{1,5},{5... | collective-permute-start | bytes 98312 | tf_op jit(solution)/shard_map/ppermute | solution.py:483
  9.4 5.8 %collective-permute-start.3 = (bf16[2,64,128]{2,1,0:T(8,128)(2,1)S(1)}, bf16[2,64,128]{2,1,0:T(8,128)(2,1)S(1)}, u32[]{:S(2)}, u32[]{:S(2)}) collective-permute-start(bf16[2,64,128]{2,1,0:T(8,128)(2,1)S(1)} %shard_map.103), channel_id=1, source_target_pairs={{0,3},{1,2},{2,1},{3,0},{4,7},{5,6},{6,5},{7,4},{8,11},{9,10},{10,... | collective-permute-start | bytes 98312 | tf_op jit(solution)/shard_map/ppermute | solution.py:469
  13.0 3.9 %collective-permute-start.2 = (bf16[2,64,128]{2,1,0:T(8,128)(2,1)S(1)}, bf16[2,64,128]{2,1,0:T(8,128)(2,1)S(1)}, u32[]{:S(2)}, u32[]{:S(2)}) collective-permute-start(bf16[2,64,128]{2,1,0:T(8,128)(2,1)S(1)} %shard_map.103), channel_id=1, source_target_pairs={{0,1},{1,0},{2,3},{3,2},{4,5},{5,4},{6,7},{7,6},{8,9},{9,8},{10,11... | collective-permute-start | bytes 98312 | tf_op jit(solution)/shard_map/ppermute | solution.py:468
  17.0 15.3 %copy-start.4 = (f32[64]{0:T(128)S(1)}, f32[64]{0:T(128)}, u32[]{:S(2)}) copy-start(f32[64]{0:T(128)} %param.9) | copy-start | bytes 772
  17.0 15.3 %copy-start.5 = (f32[64]{0:T(128)S(1)}, f32[64]{0:T(128)}, u32[]{:S(2)}) copy-start(f32[64]{0:T(128)} %param.10) | copy-start | bytes 772
  47.0 5.5 %collective-permute-start.5 = (bf16[64,128]{1,0:T(8,128)(2,1)S(1)}, bf16[64,128]{1,0:T(8,128)(2,1)S(1)}, u32[]{:S(2)}, u32[]{:S(2)}) collective-permute-start(bf16[64,128]{1,0:T(8,128)(2,1)S(1)} %get-tuple-element.54), channel_id=1, source_target_pairs={{0,3},{1,2},{2,1},{3,0},{4,7},{5,6},{6,5},{7,4},{8,11},{9,10},{10,... | collective-permute-start | bytes 49160 | tf_op jit(solution)/shard_map/ppermute | solution.py:469
  47.6 5.0 %collective-permute-start.4 = (bf16[64,128]{1,0:T(8,128)(2,1)S(1)}, bf16[64,128]{1,0:T(8,128)(2,1)S(1)}, u32[]{:S(2)}, u32[]{:S(2)}) collective-permute-start(bf16[64,128]{1,0:T(8,128)(2,1)S(1)} %get-tuple-element.54), channel_id=1, source_target_pairs={{0,1},{1,0},{2,3},{3,2},{4,5},{5,4},{6,7},{7,6},{8,9},{9,8},{10,11... | collective-permute-start | bytes 49160 | tf_op jit(solution)/shard_map/ppermute | solution.py:468
  48.1 12.3 %all-to-all-start.2 = ((f32[32,1,1152]{2,1,0:T(1,128)}), f32[32,1,1152]{2,1,0:T(1,128)S(1)}, u32[]{:S(2)}, u32[]{:S(2)}) async-start(f32[32,1,1152]{2,1,0:T(1,128)} %get-tuple-element.51), calls=%async_computation.2 | async-start | bytes 294912 | tf_op jit(solution)/shard_map/all_to_all | solution.py:566
  52.8 3.1 %collective-permute-start.7 = (bf16[3,64,128]{2,1,0:T(8,128)(2,1)S(1)}, bf16[3,64,128]{2,1,0:T(8,128)(2,1)S(1)}, u32[]{:S(2)}, u32[]{:S(2)}) collective-permute-start(bf16[3,64,128]{2,1,0:T(8,128)(2,1)S(1)} %get-tuple-element.67), channel_id=1, source_target_pairs={{4,8},{8,4},{12,16},{16,12},{20,24},{24,20},{5,9},{9,5},{13,17},{1... | collective-permute-start | bytes 147464 | tf_op jit(solution)/shard_map/ppermute | solution.py:482
  53.4 3.3 %collective-permute-start.6 = (bf16[3,64,128]{2,1,0:T(8,128)(2,1)S(1)}, bf16[3,64,128]{2,1,0:T(8,128)(2,1)S(1)}, u32[]{:S(2)}, u32[]{:S(2)}) collective-permute-start(bf16[3,64,128]{2,1,0:T(8,128)(2,1)S(1)} %get-tuple-element.68), channel_id=1, source_target_pairs={{0,4},{4,0},{8,12},{12,8},{16,20},{20,16},{24,28},{28,24},{1,5},{5... | collective-permute-start | bytes 147464 | tf_op jit(solution)/shard_map/ppermute | solution.py:483
  61.3 11.7 %all-to-all-start.3 = ((f32[32,1,1152]{2,1,0:T(1,128)}), f32[32,1,1152]{2,1,0:T(1,128)S(1)}, u32[]{:S(2)}, u32[]{:S(2)}) async-start(f32[32,1,1152]{2,1,0:T(1,128)} %broadcast_in_dim.14), calls=%async_computation.3 | async-start | bytes 294912 | tf_op jit(solution)/shard_map/all_to_all | solution.py:571
